TPU v7x, 32 devices: a whole 2x2x4 slice. The times are simulated.
32 devices in a mesh: shot: 2 (over y), box: 8 (over z, x), sub: 2 (over core).
Axes of the slice: x: 2, y: 2, z: 4, core: 2. Of those that a mesh axis runs over, the one named last changes fastest.
Arguments:
- box_weights: float32 [64, 256, 128], P(('shot', 'box', 'sub')), parts along dimension 0, may hold values from -6 to 6
- velocity: float32 [8192], P('shot'), parts along dimension 0, may hold values from -4 to 4
- switch_kernel: float32 [128, 128], replicated, may hold values from -0.5 to 0.5
Outputs:
- final_weights: float32 [4, 4096, 128], P('shot', ('box', 'sub')), parts along dimension 0
There are 2 independent parts, one for each index of `shot`. A program takes and returns all parts, laid end to end along the dimension named above; an argument that names none is the same for every part. Nothing has to cross between parts.
All inputs are finite; a program needn't handle non-finite values.
Results may differ from a plain program's by a relative error of at most 0.00013.
Values sent between devices are 32-bit elements; how exact they have to be, the bound alone decides.
No kernel may reach another device: no remote copies, remote signals or barrier semaphores. Data moves between devices by JAX's collectives and lax.ppermute only.
A program may use at most 64 MiB of HBM per device.

v0:
```python
import functools

import jax
import jax.numpy as jnp
import numpy as np
from jax import lax
from jax.experimental import pallas as pl
from jax.experimental.pallas import tpu as pltpu
from jax.sharding import PartitionSpec as P


CHEB = 8
POINTS = CHEB * CHEB
VEC = 2 * POINTS
HALF_ROOT = 0.7071067811865476
SHARES = (8, 4, 4)
EARLY = (False, False, True)
LANES = 128
KINDS = 6
VMEM_ROOM = 8 << 20


COS_SERIES = [-1.0 / 87178291200.0, 1.0 / 479001600.0, -1.0 / 3628800.0, 1.0 / 40320.0, -1.0 / 720.0, 1.0 / 24.0, -0.5, 1.0]
SIN_SERIES = [-1.0 / 1307674368000.0, 1.0 / 6227020800.0, -1.0 / 39916800.0, 1.0 / 362880.0, -1.0 / 5040.0, 1.0 / 120.0, -1.0 / 6.0, 1.0]


def nodes():
    return np.cos(np.pi * (2.0 * np.arange(CHEB) + 1.0) / (2.0 * CHEB))


def child_matrices(axis_dim):
    z = nodes()
    found = []
    for child in (0, 1):
        y = (z + (2.0 * child - 1.0)) * 0.5
        rows = np.ones((CHEB, CHEB))
        for k in range(CHEB):
            for other in range(CHEB):
                if other != k:
                    rows[:, k] *= (y - z[other]) / (z[k] - z[other])
        single = np.kron(rows, np.eye(CHEB)) if axis_dim == 0 else np.kron(np.eye(CHEB), rows)
        found.append(np.kron(np.eye(2), single).astype(np.float32))
    both = np.stack([np.concatenate(found, 0), np.concatenate(found[::-1], 0)])
    high = both.astype(jnp.bfloat16)
    low = (both - high.astype(np.float32)).astype(jnp.bfloat16)
    return np.concatenate([high, low], -1)


def cos_sin(angle):
    square = angle * angle
    c = jnp.full_like(square, COS_SERIES[0])
    for term in COS_SERIES[1:]:
        c = c * square + term
    s = jnp.full_like(square, SIN_SERIES[0])
    for term in SIN_SERIES[1:]:
        s = s * square + term
    return c, s * angle


def halves(x):
    high = x.astype(jnp.bfloat16)
    return high, (x - high.astype(jnp.float32)).astype(jnp.bfloat16)


def mm(a, b):
    return jnp.dot(a, b, preferred_element_type=jnp.float32)


def mixed_with(x, mat):
    high, low = halves(x)
    wide = mm(high, mat)
    n = wide.shape[1] // 2
    return wide[:, :n] + wide[:, n:] + mm(low, mat[:, :n])


def expand(values, spots):
    a = values.astype(jnp.bfloat16)
    rest = values - a.astype(jnp.float32)
    b = rest.astype(jnp.bfloat16)
    c = (rest - b.astype(jnp.float32)).astype(jnp.bfloat16)
    pieces = jnp.concatenate([a.astype(jnp.float32), b.astype(jnp.float32), c.astype(jnp.float32)], 0)
    return lax.dot_general(
        pieces.astype(jnp.bfloat16), spots, (((0,), (0,)), ((), ())), preferred_element_type=jnp.float32
    )


def prologue_kernel(levels, sub_count, x_hbm, vel_hbm, even_hbm, odd_hbm, sw_hbm, x_ref, even_ref, odd_ref, sw_ref, tab_ref, vel_ref, sw_in, sems):
    copies = [
        pltpu.make_async_copy(vel_hbm, vel_ref, sems.at[0]),
        pltpu.make_async_copy(x_hbm, x_ref, sems.at[1]),
        pltpu.make_async_copy(even_hbm, even_ref, sems.at[2]),
        pltpu.make_async_copy(odd_hbm, odd_ref, sems.at[3]),
        pltpu.make_async_copy(sw_hbm, sw_in, sems.at[4]),
    ]
    for copy in copies:
        copy.start()
    device = lax.axis_index("box") * sub_count + lax.axis_index("sub")
    tgt = tab_ref.shape[2]
    rows = tgt // LANES
    node = lax.broadcasted_iota(jnp.int32, (CHEB, LANES), 0)
    z = jnp.zeros((CHEB, LANES), jnp.float32)
    for k, value in enumerate(nodes()):
        z = jnp.where(node == k, float(value), z)
    node = lax.broadcasted_iota(jnp.int32, (3 * CHEB, VEC), 0) % CHEB
    lane = lax.broadcasted_iota(jnp.int32, (3 * CHEB, VEC), 1)
    sign = jnp.where(lane < POINTS, -1.0, 1.0)
    point = lane % POINTS
    spots = []
    for spot in (point // CHEB, point % CHEB):
        hit = jnp.where(spot == node, 1.0, 0.0)
        spots.append((hit.astype(jnp.bfloat16), (hit * sign).astype(jnp.bfloat16)))
    copies[0].wait()
    for entry in range(levels + 1):
        level = min(entry, levels - 1)
        code = device % 2 ** (level + 1)
        child = (device // 2**level) % 2
        if entry == levels:
            code = code + (1 - 2 * child) * 2**level
        k = 2.0 * child.astype(jnp.float32) - 1.0
        plain, signed = spots[level % 2]
        for r in range(rows):
            half = 0.5 * jnp.broadcast_to(vel_ref[pl.ds(code * rows + r, 1), :], (CHEB, LANES))
            c1, s1 = cos_sin(half * z)
            ca, sa = cos_sin(half)
            sa = sa * k
            p, q, u, t = c1 * ca, s1 * sa, s1 * ca, c1 * sa
            cosines = (p - q, p + q, (1.0 - 2.0 * s1 * s1) * HALF_ROOT)
            sines = (-(u + t), t - u, (2.0 * HALF_ROOT) * s1 * c1)
            at = slice(r * LANES, (r + 1) * LANES)
            wide = expand(jnp.concatenate(cosines, 1), plain)
            wide_s = expand(jnp.concatenate(sines, 1), signed)
            for i in range(3):
                tab_ref[entry, 2 * i, at, :] = wide[i * LANES : (i + 1) * LANES]
                tab_ref[entry, 2 * i + 1, at, :] = wide_s[i * LANES : (i + 1) * LANES]
    copies[4].wait()
    high, low = halves(sw_in[...])
    sw_ref[...] = jnp.concatenate([high, low], 1)
    for copy in copies[1:4]:
        copy.wait()


def prologue(levels, sub_count, x, vel, switch):
    tgt = x.shape[1]
    mats = [jnp.asarray(child_matrices(e)) for e in (0, 1)]
    anywhere = pl.BlockSpec(memory_space=pltpu.HBM)
    vmem = pl.BlockSpec(memory_space=pltpu.VMEM)
    return pl.pallas_call(
        functools.partial(prologue_kernel, levels, sub_count),
        out_shape=[
            jax.ShapeDtypeStruct(x.shape, jnp.float32),
            jax.ShapeDtypeStruct(mats[0].shape, jnp.bfloat16),
            jax.ShapeDtypeStruct(mats[1].shape, jnp.bfloat16),
            jax.ShapeDtypeStruct((VEC, 2 * VEC), jnp.bfloat16),
            jax.ShapeDtypeStruct((levels + 1, KINDS, tgt, VEC), jnp.float32),
        ],
        in_specs=[anywhere] * 5,
        out_specs=[vmem] * 5,
        scratch_shapes=[
            pltpu.VMEM(vel.shape, jnp.float32),
            pltpu.VMEM(switch.shape, jnp.float32),
            pltpu.SemaphoreType.DMA((5,)),
        ],
        compiler_params=pltpu.CompilerParams(vmem_limit_bytes=VMEM_ROOM),
        name="prologue",
    )(*[pltpu.with_memory_space_constraint(v, pltpu.HBM) for v in (x, vel, mats[0], mats[1], switch)])


def turn(v, c, s):
    return v * c[None] + pltpu.roll(v, POINTS, 2) * s[None]


def bit_of(sub_count, level):
    return ((lax.axis_index("box") * sub_count + lax.axis_index("sub")) // 2**level) % 2


def merged(own, far, tab_ref, entry, start, mat):
    shape = far.shape
    at = slice(start, start + shape[1])
    own = turn(own, tab_ref[entry, 0, at], tab_ref[entry, 1, at])
    far = turn(far, tab_ref[entry, 2, at], tab_ref[entry, 3, at])
    both = jnp.concatenate([own.reshape(-1, VEC), far.reshape(-1, VEC)], 1)
    mixed = mixed_with(both, mat).reshape(shape)
    return turn(mixed, tab_ref[entry, 4, at], tab_ref[entry, 5, at])


def level_value(plan, level, start, own, far, tab_ref, mat_ref, sw_ref):
    result = merged(own, far, tab_ref, level, start, mat_ref[bit_of(plan.sub_count, level)])
    if level == plan.switch_level:
        result = mixed_with(result.reshape(-1, VEC), sw_ref[...]).reshape(result.shape)
    return result


def call(kernel, args, outs, scratch=(), specs=None, out_specs=None, aliases=None):
    specs = list(specs or [VMEM_SPEC] * len(args))
    return pl.pallas_call(
        kernel,
        out_shape=[jax.ShapeDtypeStruct(s, jnp.float32) for s in outs],
        in_specs=specs,
        out_specs=out_specs or [VMEM_SPEC] * len(outs),
        scratch_shapes=list(scratch),
        input_output_aliases=aliases or {},
        compiler_params=pltpu.CompilerParams(vmem_limit_bytes=VMEM_ROOM),
    )(*args)


VMEM_SPEC = pl.BlockSpec(memory_space=pltpu.VMEM)
HBM_SPEC = pl.BlockSpec(memory_space=pltpu.HBM)


class Plan:
    def __init__(self, sub_count, levels, shape):
        self.sub_count = sub_count
        self.sub_bits = sub_count.bit_length() - 1
        self.levels = levels
        self.switch_level = levels // 2 - 1
        self.src, self.tgt, _ = shape
        total = sum(SHARES)
        self.widths = [self.tgt * n // total for n in SHARES]
        self.starts = [sum(self.widths[:c]) for c in range(len(SHARES))]

    def far_of(self, value, level):
        if level < self.sub_bits:
            return swapped(value, "sub", level)
        return swapped(value, "box", level - self.sub_bits)


def first_step(plan, x, far, tab, mat, sw):
    half = plan.src // 2

    def kernel(x_ref, far_ref, tab_ref, mat_ref, sw_ref, *outs):
        result = level_value(plan, 0, 0, x_ref[...], far_ref[...], tab_ref, mat_ref, sw_ref)
        upper = bit_of(plan.sub_count, plan.levels - 1) == 1
        outs = list(outs)
        for start, width, early in zip(plan.starts, plan.widths, EARLY):
            part = result[:, start : start + width]
            if early:
                outs.pop(0)[...] = jnp.where(upper, part[half:], part[:half])
                outs.pop(0)[...] = jnp.where(upper, part[:half], part[half:])
            else:
                outs.pop(0)[...] = part

    outs = []
    for width, early in zip(plan.widths, EARLY):
        outs += [(half, width, VEC)] * 2 if early else [(plan.src, width, VEC)]
    outs = list(call(kernel, [x, far, tab, mat, sw], outs))
    return [(outs.pop(0), outs.pop(0)) if early else (outs.pop(0),) for early in EARLY]


def step(plan, level, c, own, far, tab, mat, sw):
    def kernel(own_ref, far_ref, tab_ref, mat_ref, sw_ref, *rest):
        rest[-1][...] = level_value(plan, level, plan.starts[c], own_ref[...], far_ref[...], tab_ref, mat_ref, sw_ref)

    return call(kernel, [own, far, tab, mat, sw], [own.shape])[0]


def join(kept, received):
    def kernel(a_ref, b_ref, *rest):
        n = a_ref.shape[0]
        rest[-1][:n] = a_ref[...]
        rest[-1][n:] = b_ref[...]

    return call(kernel, [kept, received], [(2 * kept.shape[0], *kept.shape[1:])])[0]


def early_end(plan, c, own, far, tab, mats, sw):
    last = plan.levels - 1
    start = plan.starts[c]

    def kernel(own_ref, far_ref, tab_ref, mat_ref, last_mat_ref, sw_ref, mine_ref, theirs_ref):
        x = level_value(plan, last - 1, start, own_ref[...], far_ref[...], tab_ref, mat_ref, sw_ref)
        half = x.shape[0] // 2
        mat = last_mat_ref[bit_of(plan.sub_count, last)]
        theirs_ref[...] = merged(x[:half], x[half:], tab_ref, last + 1, start, mat)
        mine_ref[...] = merged(x[:half], x[half:], tab_ref, last, start, mat)

    shape = (own.shape[0] // 2, *own.shape[1:])
    return call(kernel, [own, far, tab, mats[(last - 1) % 2], mats[last % 2], sw], [shape, shape])


def finish(plan, results):
    flat = [part for result in results for part in result]

    def kernel(*refs):
        parts, out_hbm, sems = list(refs[: len(flat)]), refs[-2], refs[-1]
        upper = bit_of(plan.sub_count, plan.levels - 1)
        copies = []
        for start, result in zip(plan.starts, results):
            for i in range(len(result)):
                ref = parts.pop(0)
                rows, count, _ = ref.shape
                box = 0 if len(result) == 1 else (upper if i == 0 else 1 - upper) * rows
                place = out_hbm.at[pl.ds(box, rows), pl.ds(start, count)]
                copies.append(pltpu.make_async_copy(ref, place, sems.at[len(copies)]))
        for copy in copies:
            copy.start()
        for copy in copies:
            copy.wait()

    scratch = [pltpu.SemaphoreType.DMA((len(flat),))]
    return call(kernel, flat, [(plan.src, plan.tgt, VEC)], scratch, None, [HBM_SPEC])[0]


def swapped(value, axis, apart):
    mask = 2**apart
    pairs = [(source, source ^ mask) for source in range(lax.axis_size(axis))]
    return lax.ppermute(value, axis, pairs)


def levels_of(box_weights, velocity, switch_kernel):
    sub_count = lax.axis_size("sub")
    levels = lax.axis_size("box").bit_length() - 1 + sub_count.bit_length() - 1
    plan = Plan(sub_count, levels, box_weights.shape)
    last = levels - 1

    far = plan.far_of(box_weights, 0)
    x, even, odd, sw, tab = prologue(levels, sub_count, box_weights, velocity.reshape(-1, LANES), switch_kernel)
    mats = (even, odd)
    parts = first_step(plan, x, far, tab, mats[0], sw)
    results = []
    for c, (part, *leaving) in enumerate(parts):
        early = bool(leaving)
        if early:
            received = plan.far_of(leaving[0], last)
            part = join(part, received)
        for level in range(1, last - 1 if early else levels):
            far = plan.far_of(part, level)
            part = step(plan, level, c, part, far, tab, mats[level % 2], sw)
        if early:
            far = plan.far_of(part, last - 1)
            mine, theirs = early_end(plan, c, part, far, tab, mats, sw)
            results.append((mine, plan.far_of(theirs, last)))
        else:
            results.append((part,))
    return finish(plan, results)


def solution(mesh):
    return jax.shard_map(
        levels_of,
        mesh=mesh,
        in_specs=(P(("shot", "box", "sub"), None, None), P("shot"), P()),
        out_specs=P("shot", ("box", "sub"), None),
        check_vma=False,
    )
```

profile of v0, /device:TPU:0, one launch (start us, length us, event | category | flops | bytes accessed | tf_op | source)
XLA Modules:
  0.0 32.9 jit_solution(7655422280802869619)
XLA Ops:
  0.0 0.5 %collective-permute-start = (f32[2,256,128]{2,1,0:T(8,128)}, f32[2,256,128]{2,1,0:T(8,128)S(1)}, u32[]{:S(2)}, u32[]{:S(2)}) collective-permute-start(f32[2,256,128]{2,1,0:T(8,128)} %x_hbm.1), channel_id=1, source_target_pairs={{0,1},{1,0},{2,3},{3,2},{4,5},{5,4},{6,7},{7,6},{8,9},{9,8},{10,11... | collective-permute-start | bytes 786440 | tf_op jit(solution)/shard_map/ppermute | solution.py:306
  0.5 1.5 %prologue.1 = (f32[2,256,128]{2,1,0:T(8,128)S(1)}, bf16[2,256,256]{2,1,0:T(8,128)(2,1)S(1)}, bf16[2,256,256]{2,1,0:T(8,128)(2,1)S(1)}, bf16[128,256]{1,0:T(8,128)(2,1)S(1)}, f32[5,6,256,128]{3,2,1,0:T(8,128)S(1)}) custom-call(f32[2,256,128]{2,1,0:T(8,128)} %x_hbm.1, f32[32,128]{1,0:T(8,128)} %bitcast.1, bf16[2,256,256]{2,1,0:T(8,128)(2,1)} %constant.4.clone.even_hbm, ...), custom_call_target="tpu_custom_call" | custom-call | tf_op jit(solution)/shard_map/prologue/pallas_call | solution.py:147
  2.0 0.0 collective-permute-done.far_ref
  2.0 0.4 %shard_map.55 = (f32[2,128,128]{2,1,0:T(8,128)S(1)}, f32[2,64,128]{2,1,0:T(8,128)S(1)}, f32[1,64,128]{2,1,0:T(8,128)S(1)}, f32[1,64,128]{2,1,0:T(8,128)S(1)}) custom-call(f32[2,256,128]{2,1,0:T(8,128)S(1)} %get-tuple-element.16.x_ref, f32[2,256,128]{2,1,0:T(8,128)S(1)} %collective-permute-done.far_ref, f32[5,6,256,128]{3,2,1,0:T(8,128)S(1)} %get-tuple-element.17.tab_ref, ...), custom_call_target="tpu_custom_call" | custom-call | tf_op jit(solution)/shard_map/pallas_call | solution.py:195
  2.5 2.7 %collective-permute-start.1 = (f32[2,128,128]{2,1,0:T(8,128)S(1)}, f32[2,128,128]{2,1,0:T(8,128)S(1)}, u32[]{:S(2)}, u32[]{:S(2)}) collective-permute-start(f32[2,128,128]{2,1,0:T(8,128)S(1)} %get-tuple-element.20.own_ref), channel_id=1, source_target_pairs={{0,2},{2,0},{4,6},{6,4},{8,10},{10,8},{12,14},{14,12},{1,3},{3,1},... | collective-permute-start | bytes 393224 | tf_op jit(solution)/shard_map/ppermute | solution.py:306
  5.2 4.0 %collective-permute-done.1.far_ref = f32[2,128,128]{2,1,0:T(8,128)S(1)} collective-permute-done((f32[2,128,128]{2,1,0:T(8,128)S(1)}, f32[2,128,128]{2,1,0:T(8,128)S(1)}, u32[]{:S(2)}, u32[]{:S(2)}) %collective-permute-start.1) | collective-permute-done | bytes 131104 | tf_op jit(solution)/shard_map/ppermute | solution.py:306
  9.2 0.5 %shard_map.56.own_ref = f32[2,128,128]{2,1,0:T(8,128)S(1)} custom-call(f32[2,128,128]{2,1,0:T(8,128)S(1)} %get-tuple-element.20.own_ref, f32[2,128,128]{2,1,0:T(8,128)S(1)} %collective-permute-done.1.far_ref, f32[5,6,256,128]{3,2,1,0:T(8,128)S(1)} %get-tuple-element.17.tab_ref, bf16[2,256,256]{2,1,0:T(8,128)(2,1)S(1)} %get-tuple-element.21.mat_ref.last_mat_ref, ...), custom_call_target="tpu_custom_call" | custom-call | tf_op jit(solution)/shard_map/pallas_call | solution.py:195
  9.7 1.9 %collective-permute-start.2 = (f32[2,128,128]{2,1,0:T(8,128)S(1)}, f32[2,128,128]{2,1,0:T(8,128)S(1)}, u32[]{:S(2)}, u32[]{:S(2)}) collective-permute-start(f32[2,128,128]{2,1,0:T(8,128)S(1)} %shard_map.56.own_ref), channel_id=1, source_target_pairs={{0,4},{2,6},{4,0},{6,2},{8,12},{10,14},{12,8},{14,10},{1,5},{3,7},... | collective-permute-start | bytes 393224 | tf_op jit(solution)/shard_map/ppermute | solution.py:306
  11.6 2.6 %collective-permute-start.7 = (f32[1,64,128]{2,1,0:T(8,128)S(1)}, f32[1,64,128]{2,1,0:T(8,128)S(1)}, u32[]{:S(2)}, u32[]{:S(2)}) collective-permute-start(f32[1,64,128]{2,1,0:T(8,128)S(1)} %get-tuple-element.24), channel_id=1, source_target_pairs={{0,8},{2,10},{4,12},{6,14},{8,0},{10,2},{12,4},{14,6},{1,9},{3,11}... | collective-permute-start | bytes 98312 | tf_op jit(solution)/shard_map/ppermute | solution.py:306
  14.1 1.5 %collective-permute-start.4 = (f32[2,64,128]{2,1,0:T(8,128)S(1)}, f32[2,64,128]{2,1,0:T(8,128)S(1)}, u32[]{:S(2)}, u32[]{:S(2)}) collective-permute-start(f32[2,64,128]{2,1,0:T(8,128)S(1)} %get-tuple-element.22.own_ref), channel_id=1, source_target_pairs={{0,2},{2,0},{4,6},{6,4},{8,10},{10,8},{12,14},{14,12},{1,3},{3,1},... | collective-permute-start | bytes 196616 | tf_op jit(solution)/shard_map/ppermute | solution.py:306
  15.6 0.8 %collective-permute-done.7.b_ref = f32[1,64,128]{2,1,0:T(8,128)S(1)} collective-permute-done((f32[1,64,128]{2,1,0:T(8,128)S(1)}, f32[1,64,128]{2,1,0:T(8,128)S(1)}, u32[]{:S(2)}, u32[]{:S(2)}) %collective-permute-start.7) | collective-permute-done | bytes 32800 | tf_op jit(solution)/shard_map/ppermute | solution.py:306
  16.4 1.5 %collective-permute-start.8 = (f32[2,64,128]{2,1,0:T(8,128)S(1)}, f32[2,64,128]{2,1,0:T(8,128)S(1)}, u32[]{:S(2)}, u32[]{:S(2)}) collective-permute-start(f32[2,64,128]{2,1,0:T(8,128)S(1)} %shard_map.62.own_ref), channel_id=1, source_target_pairs={{0,2},{2,0},{4,6},{6,4},{8,10},{10,8},{12,14},{14,12},{1,3},{3,1},... | collective-permute-start | bytes 196616 | tf_op jit(solution)/shard_map/ppermute | solution.py:306
  17.9 0.6 %collective-permute-done.4.far_ref = f32[2,64,128]{2,1,0:T(8,128)S(1)} collective-permute-done((f32[2,64,128]{2,1,0:T(8,128)S(1)}, f32[2,64,128]{2,1,0:T(8,128)S(1)}, u32[]{:S(2)}, u32[]{:S(2)}) %collective-permute-start.4) | collective-permute-done | bytes 65568 | tf_op jit(solution)/shard_map/ppermute | solution.py:306
  18.5 0.4 %shard_map.59.own_ref = f32[2,64,128]{2,1,0:T(8,128)S(1)} custom-call(f32[2,64,128]{2,1,0:T(8,128)S(1)} %get-tuple-element.22.own_ref, f32[2,64,128]{2,1,0:T(8,128)S(1)} %collective-permute-done.4.far_ref, f32[5,6,256,128]{3,2,1,0:T(8,128)S(1)} %get-tuple-element.17.tab_ref, bf16[2,256,256]{2,1,0:T(8,128)(2,1)S(1)} %get-tuple-element.21.mat_ref.last_mat_ref, ...), custom_call_target="tpu_custom_call" | custom-call | tf_op jit(solution)/shard_map/pallas_call | solution.py:195
  18.9 1.2 %collective-permute-start.5 = (f32[2,64,128]{2,1,0:T(8,128)S(1)}, f32[2,64,128]{2,1,0:T(8,128)S(1)}, u32[]{:S(2)}, u32[]{:S(2)}) collective-permute-start(f32[2,64,128]{2,1,0:T(8,128)S(1)} %shard_map.59.own_ref), channel_id=1, source_target_pairs={{0,4},{2,6},{4,0},{6,2},{8,12},{10,14},{12,8},{14,10},{1,5},{3,7},... | collective-permute-start | bytes 196616 | tf_op jit(solution)/shard_map/ppermute | solution.py:306
  20.1 0.0 collective-permute-done.2.far_ref
  20.1 0.3 %shard_map.57.own_ref = f32[2,128,128]{2,1,0:T(8,128)S(1)} custom-call(f32[2,128,128]{2,1,0:T(8,128)S(1)} %shard_map.56.own_ref, f32[2,128,128]{2,1,0:T(8,128)S(1)} %collective-permute-done.2.far_ref, f32[5,6,256,128]{3,2,1,0:T(8,128)S(1)} %get-tuple-element.17.tab_ref, bf16[2,256,256]{2,1,0:T(8,128)(2,1)S(1)} %get-tuple-element.18.mat_ref, ...), custom_call_target="tpu_custom_call" | custom-call | tf_op jit(solution)/shard_map/pallas_call | solution.py:195
  20.5 1.4 %collective-permute-start.3 = (f32[2,128,128]{2,1,0:T(8,128)S(1)}, f32[2,128,128]{2,1,0:T(8,128)S(1)}, u32[]{:S(2)}, u32[]{:S(2)}) collective-permute-start(f32[2,128,128]{2,1,0:T(8,128)S(1)} %shard_map.57.own_ref), channel_id=1, source_target_pairs={{0,8},{2,10},{4,12},{6,14},{8,0},{10,2},{12,4},{14,6},{1,9},{3,11}... | collective-permute-start | bytes 393224 | tf_op jit(solution)/shard_map/ppermute | solution.py:306
  21.9 0.0 collective-permute-done.8.far_ref
  21.9 0.4 %shard_map.63.own_ref = f32[2,64,128]{2,1,0:T(8,128)S(1)} custom-call(f32[2,64,128]{2,1,0:T(8,128)S(1)} %shard_map.62.own_ref, f32[2,64,128]{2,1,0:T(8,128)S(1)} %collective-permute-done.8.far_ref, f32[5,6,256,128]{3,2,1,0:T(8,128)S(1)} %get-tuple-element.17.tab_ref, bf16[2,256,256]{2,1,0:T(8,128)(2,1)S(1)} %get-tuple-element.21.mat_ref.last_mat_ref, ...), custom_call_target="tpu_custom_call" | custom-call | tf_op jit(solution)/shard_map/pallas_call | solution.py:195
  22.4 1.5 %collective-permute-start.9 = (f32[2,64,128]{2,1,0:T(8,128)S(1)}, f32[2,64,128]{2,1,0:T(8,128)S(1)}, u32[]{:S(2)}, u32[]{:S(2)}) collective-permute-start(f32[2,64,128]{2,1,0:T(8,128)S(1)} %shard_map.63.own_ref), channel_id=1, source_target_pairs={{0,4},{2,6},{4,0},{6,2},{8,12},{10,14},{12,8},{14,10},{1,5},{3,7},... | collective-permute-start | bytes 196616 | tf_op jit(solution)/shard_map/ppermute | solution.py:306
  23.9 0.9 %collective-permute-done.5.far_ref = f32[2,64,128]{2,1,0:T(8,128)S(1)} collective-permute-done((f32[2,64,128]{2,1,0:T(8,128)S(1)}, f32[2,64,128]{2,1,0:T(8,128)S(1)}, u32[]{:S(2)}, u32[]{:S(2)}) %collective-permute-start.5) | collective-permute-done | bytes 65568 | tf_op jit(solution)/shard_map/ppermute | solution.py:306
  24.8 0.3 shard_map.60.own_ref
  25.1 0.9 %collective-permute-start.6 = (f32[2,64,128]{2,1,0:T(8,128)S(1)}, f32[2,64,128]{2,1,0:T(8,128)S(1)}, u32[]{:S(2)}, u32[]{:S(2)}) collective-permute-start(f32[2,64,128]{2,1,0:T(8,128)S(1)} %shard_map.60.own_ref), channel_id=1, source_target_pairs={{0,8},{2,10},{4,12},{6,14},{8,0},{10,2},{12,4},{14,6},{1,9},{3,11}... | collective-permute-start | bytes 196616 | tf_op jit(solution)/shard_map/ppermute | solution.py:306
  26.0 0.7 %collective-permute-done.9.far_ref = f32[2,64,128]{2,1,0:T(8,128)S(1)} collective-permute-done((f32[2,64,128]{2,1,0:T(8,128)S(1)}, f32[2,64,128]{2,1,0:T(8,128)S(1)}, u32[]{:S(2)}, u32[]{:S(2)}) %collective-permute-start.9) | collective-permute-done | bytes 65568 | tf_op jit(solution)/shard_map/ppermute | solution.py:306
  26.7 0.6 %shard_map.64 = (f32[1,64,128]{2,1,0:T(8,128)S(1)}, f32[1,64,128]{2,1,0:T(8,128)S(1)}) custom-call(f32[2,64,128]{2,1,0:T(8,128)S(1)} %shard_map.63.own_ref, f32[2,64,128]{2,1,0:T(8,128)S(1)} %collective-permute-done.9.far_ref, f32[5,6,256,128]{3,2,1,0:T(8,128)S(1)} %get-tuple-element.17.tab_ref, bf16[2,256,256]{2,1,0:T(8,128)(2,1)S(1)} %get-tuple-element.18.mat_ref, ...), custom_call_target="tpu_custom_call" | custom-call | tf_op jit(solution)/shard_map/pallas_call | solution.py:195
  27.3 1.7 %collective-permute-start.10 = (f32[1,64,128]{2,1,0:T(8,128)S(1)}, f32[1,64,128]{2,1,0:T(8,128)S(1)}, u32[]{:S(2)}, u32[]{:S(2)}) collective-permute-start(f32[1,64,128]{2,1,0:T(8,128)S(1)} %get-tuple-element.26), channel_id=1, source_target_pairs={{0,8},{2,10},{4,12},{6,14},{8,0},{10,2},{12,4},{14,6},{1,9},{3,11}... | collective-permute-start | bytes 98312 | tf_op jit(solution)/shard_map/ppermute | solution.py:306
  29.0 2.2 %collective-permute-done.6.far_ref = f32[2,64,128]{2,1,0:T(8,128)S(1)} collective-permute-done((f32[2,64,128]{2,1,0:T(8,128)S(1)}, f32[2,64,128]{2,1,0:T(8,128)S(1)}, u32[]{:S(2)}, u32[]{:S(2)}) %collective-permute-start.6) | collective-permute-done | bytes 65568 | tf_op jit(solution)/shard_map/ppermute | solution.py:306
  31.2 0.3 shard_map.61.refs_1_
  31.5 0.0 collective-permute-done.3.far_ref
  31.5 0.3 %shard_map.58.refs_0_ = f32[2,128,128]{2,1,0:T(8,128)S(1)} custom-call(f32[2,128,128]{2,1,0:T(8,128)S(1)} %shard_map.57.own_ref, f32[2,128,128]{2,1,0:T(8,128)S(1)} %collective-permute-done.3.far_ref, f32[5,6,256,128]{3,2,1,0:T(8,128)S(1)} %get-tuple-element.17.tab_ref, bf16[2,256,256]{2,1,0:T(8,128)(2,1)S(1)} %get-tuple-element.21.mat_ref.last_mat_ref, ...), custom_call_target="tpu_custom_call" | custom-call | tf_op jit(solution)/shard_map/pallas_call | solution.py:195
  31.9 0.3 collective-permute-done.10.refs_3_
  32.2 0.7 %shard_map.65 = f32[2,256,128]{2,1,0:T(8,128)} custom-call(f32[2,128,128]{2,1,0:T(8,128)S(1)} %shard_map.58.refs_0_, f32[2,64,128]{2,1,0:T(8,128)S(1)} %shard_map.61.refs_1_, f32[1,64,128]{2,1,0:T(8,128)S(1)} %get-tuple-element.25.refs_2_, f32[1,64,128]{2,1,0:T(8,128)S(1)} %collective-permute-done.10.refs_3_), custom_call_target="tpu_custom_call" | custom-call | tf_op jit(solution)/shard_map/pallas_call | solution.py:195
  (1 shorter events, 0.0 us)
Async XLA Ops:
  0.0 2.0 %collective-permute-start = (f32[2,256,128]{2,1,0:T(8,128)}, f32[2,256,128]{2,1,0:T(8,128)S(1)}, u32[]{:S(2)}, u32[]{:S(2)}) collective-permute-start(f32[2,256,128]{2,1,0:T(8,128)} %x_hbm.1), channel_id=1, source_target_pairs={{0,1},{1,0},{2,3},{3,2},{4,5},{5,4},{6,7},{7,6},{8,9},{9,8},{10,11... | collective-permute-start | bytes 786440 | tf_op jit(solution)/shard_map/ppermute | solution.py:306
  2.5 6.7 %collective-permute-start.1 = (f32[2,128,128]{2,1,0:T(8,128)S(1)}, f32[2,128,128]{2,1,0:T(8,128)S(1)}, u32[]{:S(2)}, u32[]{:S(2)}) collective-permute-start(f32[2,128,128]{2,1,0:T(8,128)S(1)} %get-tuple-element.20.own_ref), channel_id=1, source_target_pairs={{0,2},{2,0},{4,6},{6,4},{8,10},{10,8},{12,14},{14,12},{1,3},{3,1},... | collective-permute-start | bytes 393224 | tf_op jit(solution)/shard_map/ppermute | solution.py:306
  9.7 10.5 %collective-permute-start.2 = (f32[2,128,128]{2,1,0:T(8,128)S(1)}, f32[2,128,128]{2,1,0:T(8,128)S(1)}, u32[]{:S(2)}, u32[]{:S(2)}) collective-permute-start(f32[2,128,128]{2,1,0:T(8,128)S(1)} %shard_map.56.own_ref), channel_id=1, source_target_pairs={{0,4},{2,6},{4,0},{6,2},{8,12},{10,14},{12,8},{14,10},{1,5},{3,7},... | collective-permute-start | bytes 393224 | tf_op jit(solution)/shard_map/ppermute | solution.py:306
  11.6 4.8 %collective-permute-start.7 = (f32[1,64,128]{2,1,0:T(8,128)S(1)}, f32[1,64,128]{2,1,0:T(8,128)S(1)}, u32[]{:S(2)}, u32[]{:S(2)}) collective-permute-start(f32[1,64,128]{2,1,0:T(8,128)S(1)} %get-tuple-element.24), channel_id=1, source_target_pairs={{0,8},{2,10},{4,12},{6,14},{8,0},{10,2},{12,4},{14,6},{1,9},{3,11}... | collective-permute-start | bytes 98312 | tf_op jit(solution)/shard_map/ppermute | solution.py:306
  14.1 4.4 %collective-permute-start.4 = (f32[2,64,128]{2,1,0:T(8,128)S(1)}, f32[2,64,128]{2,1,0:T(8,128)S(1)}, u32[]{:S(2)}, u32[]{:S(2)}) collective-permute-start(f32[2,64,128]{2,1,0:T(8,128)S(1)} %get-tuple-element.22.own_ref), channel_id=1, source_target_pairs={{0,2},{2,0},{4,6},{6,4},{8,10},{10,8},{12,14},{14,12},{1,3},{3,1},... | collective-permute-start | bytes 196616 | tf_op jit(solution)/shard_map/ppermute | solution.py:306
  16.4 5.5 %collective-permute-start.8 = (f32[2,64,128]{2,1,0:T(8,128)S(1)}, f32[2,64,128]{2,1,0:T(8,128)S(1)}, u32[]{:S(2)}, u32[]{:S(2)}) collective-permute-start(f32[2,64,128]{2,1,0:T(8,128)S(1)} %shard_map.62.own_ref), channel_id=1, source_target_pairs={{0,2},{2,0},{4,6},{6,4},{8,10},{10,8},{12,14},{14,12},{1,3},{3,1},... | collective-permute-start | bytes 196616 | tf_op jit(solution)/shard_map/ppermute | solution.py:306
  18.9 5.8 %collective-permute-start.5 = (f32[2,64,128]{2,1,0:T(8,128)S(1)}, f32[2,64,128]{2,1,0:T(8,128)S(1)}, u32[]{:S(2)}, u32[]{:S(2)}) collective-permute-start(f32[2,64,128]{2,1,0:T(8,128)S(1)} %shard_map.59.own_ref), channel_id=1, source_target_pairs={{0,4},{2,6},{4,0},{6,2},{8,12},{10,14},{12,8},{14,10},{1,5},{3,7},... | collective-permute-start | bytes 196616 | tf_op jit(solution)/shard_map/ppermute | solution.py:306
  20.5 11.0 %collective-permute-start.3 = (f32[2,128,128]{2,1,0:T(8,128)S(1)}, f32[2,128,128]{2,1,0:T(8,128)S(1)}, u32[]{:S(2)}, u32[]{:S(2)}) collective-permute-start(f32[2,128,128]{2,1,0:T(8,128)S(1)} %shard_map.57.own_ref), channel_id=1, source_target_pairs={{0,8},{2,10},{4,12},{6,14},{8,0},{10,2},{12,4},{14,6},{1,9},{3,11}... | collective-permute-start | bytes 393224 | tf_op jit(solution)/shard_map/ppermute | solution.py:306
  22.4 4.3 %collective-permute-start.9 = (f32[2,64,128]{2,1,0:T(8,128)S(1)}, f32[2,64,128]{2,1,0:T(8,128)S(1)}, u32[]{:S(2)}, u32[]{:S(2)}) collective-permute-start(f32[2,64,128]{2,1,0:T(8,128)S(1)} %shard_map.63.own_ref), channel_id=1, source_target_pairs={{0,4},{2,6},{4,0},{6,2},{8,12},{10,14},{12,8},{14,10},{1,5},{3,7},... | collective-permute-start | bytes 196616 | tf_op jit(solution)/shard_map/ppermute | solution.py:306
  25.1 6.1 %collective-permute-start.6 = (f32[2,64,128]{2,1,0:T(8,128)S(1)}, f32[2,64,128]{2,1,0:T(8,128)S(1)}, u32[]{:S(2)}, u32[]{:S(2)}) collective-permute-start(f32[2,64,128]{2,1,0:T(8,128)S(1)} %shard_map.60.own_ref), channel_id=1, source_target_pairs={{0,8},{2,10},{4,12},{6,14},{8,0},{10,2},{12,4},{14,6},{1,9},{3,11}... | collective-permute-start | bytes 196616 | tf_op jit(solution)/shard_map/ppermute | solution.py:306
  27.3 4.9 %collective-permute-start.10 = (f32[1,64,128]{2,1,0:T(8,128)S(1)}, f32[1,64,128]{2,1,0:T(8,128)S(1)}, u32[]{:S(2)}, u32[]{:S(2)}) collective-permute-start(f32[1,64,128]{2,1,0:T(8,128)S(1)} %get-tuple-element.26), channel_id=1, source_target_pairs={{0,8},{2,10},{4,12},{6,14},{8,0},{10,2},{12,4},{14,6},{1,9},{3,11}... | collective-permute-start | bytes 98312 | tf_op jit(solution)/shard_map/ppermute | solution.py:306
where the time goes:
time: 33.1 us; the launch traced here: 32.9 us
  starting transfers between devices  17.5 us (53%)
  waiting for transfers between devices  9.47 us (29%)
  Pallas kernels  5.9 us (18%)
    ppermute x11, starting transfers between devices, swapped(): return lax.ppermute(value, axis, pairs)  17.5 us
    ppermute x11, waiting for transfers between devices, swapped(): return lax.ppermute(value, axis, pairs)  9.47 us
    pallas_call x11, Pallas kernels, call(): pl.pallas_call(kernel, out_shape=[jax.ShapeDtypeStruct(s, jnp.float32) fo...  4.37 us
    pallas_call x1, Pallas kernels, prologue(): pl.pallas_call(functools.partial(prologue_kernel, levels, sub_count), out...  1.53 us
  transfers between devices with their start and end apart: 11, of which 7 were waited for; matrix products, arithmetic and copies ran while one was open for 0% of the time, Pallas kernels for 13%

commit v1 on v0

--- a/solution.py
+++ b/solution.py
@@ -13,10 +13,11 @@
 POINTS = CHEB * CHEB
 VEC = 2 * POINTS
 HALF_ROOT = 0.7071067811865476
-SHARES = (8, 4, 4)
-EARLY = (False, False, True)
+SHARES = (6, 5, 5)
+PLAIN, SPLIT, DOUBLE = range(3)
+KIND = (PLAIN, PLAIN, DOUBLE)
 LANES = 128
-KINDS = 6
+ENTRIES = 6
 VMEM_ROOM = 8 << 20
 
 
@@ -68,9 +69,9 @@
 
 def mixed_with(x, mat):
     high, low = halves(x)
-    wide = mm(high, mat)
-    n = wide.shape[1] // 2
-    return wide[:, :n] + wide[:, n:] + mm(low, mat[:, :n])
+    m, n = x.shape[0], mat.shape[1] // 2
+    wide = mm(jnp.concatenate([high, low], 0), mat)
+    return (wide[:m, :n] + wide[m:, :n]) + (wide[:m, n:] + wide[m:, n:])
 
 
 def expand(values, spots):
@@ -151,7 +152,7 @@
             jax.ShapeDtypeStruct(mats[0].shape, jnp.bfloat16),
             jax.ShapeDtypeStruct(mats[1].shape, jnp.bfloat16),
             jax.ShapeDtypeStruct((VEC, 2 * VEC), jnp.bfloat16),
-            jax.ShapeDtypeStruct((levels + 1, KINDS, tgt, VEC), jnp.float32),
+            jax.ShapeDtypeStruct((levels + 1, ENTRIES, tgt, VEC), jnp.float32),
         ],
         in_specs=[anywhere] * 5,
         out_specs=[vmem] * 5,
@@ -231,19 +232,19 @@
         result = level_value(plan, 0, 0, x_ref[...], far_ref[...], tab_ref, mat_ref, sw_ref)
         upper = bit_of(plan.sub_count, plan.levels - 1) == 1
         outs = list(outs)
-        for start, width, early in zip(plan.starts, plan.widths, EARLY):
+        for start, width, kind in zip(plan.starts, plan.widths, KIND):
             part = result[:, start : start + width]
-            if early:
+            if kind == SPLIT:
                 outs.pop(0)[...] = jnp.where(upper, part[half:], part[:half])
                 outs.pop(0)[...] = jnp.where(upper, part[:half], part[half:])
             else:
                 outs.pop(0)[...] = part
 
     outs = []
-    for width, early in zip(plan.widths, EARLY):
-        outs += [(half, width, VEC)] * 2 if early else [(plan.src, width, VEC)]
+    for width, kind in zip(plan.widths, KIND):
+        outs += [(half, width, VEC)] * 2 if kind == SPLIT else [(plan.src, width, VEC)]
     outs = list(call(kernel, [x, far, tab, mat, sw], outs))
-    return [(outs.pop(0), outs.pop(0)) if early else (outs.pop(0),) for early in EARLY]
+    return [(outs.pop(0), outs.pop(0)) if kind == SPLIT else (outs.pop(0),) for kind in KIND]
 
 
 def step(plan, level, c, own, far, tab, mat, sw):
@@ -266,15 +267,16 @@
     last = plan.levels - 1
     start = plan.starts[c]
 
-    def kernel(own_ref, far_ref, tab_ref, mat_ref, last_mat_ref, sw_ref, mine_ref, theirs_ref):
+    def kernel(own_ref, far_ref, tab_ref, mat_ref, last_mat_ref, sw_ref, mine_ref, *theirs):
         x = level_value(plan, last - 1, start, own_ref[...], far_ref[...], tab_ref, mat_ref, sw_ref)
         half = x.shape[0] // 2
         mat = last_mat_ref[bit_of(plan.sub_count, last)]
-        theirs_ref[...] = merged(x[:half], x[half:], tab_ref, last + 1, start, mat)
+        for ref in theirs:
+            ref[...] = merged(x[:half], x[half:], tab_ref, last + 1, start, mat)
         mine_ref[...] = merged(x[:half], x[half:], tab_ref, last, start, mat)
 
     shape = (own.shape[0] // 2, *own.shape[1:])
-    return call(kernel, [own, far, tab, mats[(last - 1) % 2], mats[last % 2], sw], [shape, shape])
+    return call(kernel, [own, far, tab, mats[(last - 1) % 2], mats[last % 2], sw], [shape] * (1 + (KIND[c] == SPLIT)))
 
 
 def finish(plan, results):
@@ -318,19 +320,18 @@
     parts = first_step(plan, x, far, tab, mats[0], sw)
     results = []
     for c, (part, *leaving) in enumerate(parts):
-        early = bool(leaving)
-        if early:
-            received = plan.far_of(leaving[0], last)
+        if KIND[c] != PLAIN:
+            received = plan.far_of((leaving or [part])[0], last)
             part = join(part, received)
-        for level in range(1, last - 1 if early else levels):
+        for level in range(1, levels if KIND[c] == PLAIN else last - 1):
             far = plan.far_of(part, level)
             part = step(plan, level, c, part, far, tab, mats[level % 2], sw)
-        if early:
-            far = plan.far_of(part, last - 1)
-            mine, theirs = early_end(plan, c, part, far, tab, mats, sw)
-            results.append((mine, plan.far_of(theirs, last)))
-        else:
+        if KIND[c] == PLAIN:
             results.append((part,))
+            continue
+        far = plan.far_of(part, last - 1)
+        mine, *theirs = early_end(plan, c, part, far, tab, mats, sw)
+        results.append((mine, *[plan.far_of(sent, last) for sent in theirs]))
     return finish(plan, results)
 
 

time: 33.1 us -> 38.8 us (1.17)
  waiting for transfers between devices: 9.47 us -> 16.1 us
  starting transfers between devices: 17.5 us -> 16.1 us
  Pallas kernels: 5.9 us -> 6.32 us
    ppermute x11 -> x10, waiting for transfers between devices: 9.47 us -> 16.1 us  [swapped(): return lax.ppermute(value, axis, pairs)]
    ppermute x11 -> x10, starting transfers between devices: 17.5 us -> 16.1 us  [swapped(): return lax.ppermute(value, axis, pairs)]
    pallas_call x11, Pallas kernels: 4.37 us -> 4.79 us  [call(): pl.pallas_call(kernel, out_shape=[jax.ShapeDtypeStruct(s, jnp.float32) fo...]
  transfers between devices with their start and end apart: 11 -> 10, of which waited for: 7 -> 4; matrix products, arithmetic and copies ran while one was open for 0% -> 0% of each run, Pallas kernels for 13% -> 12%
where the time goes in v1:
time: 38.8 us; the launch traced here: 38.6 us
  starting transfers between devices  16.1 us (41%)
  waiting for transfers between devices  16.1 us (41%)
  Pallas kernels  6.32 us (16%)
    ppermute x10, starting transfers between devices, swapped(): return lax.ppermute(value, axis, pairs)  16.1 us
    ppermute x10, waiting for transfers between devices, swapped(): return lax.ppermute(value, axis, pairs)  16.1 us
    pallas_call x11, Pallas kernels, call(): pl.pallas_call(kernel, out_shape=[jax.ShapeDtypeStruct(s, jnp.float32) fo...  4.79 us
    pallas_call x1, Pallas kernels, prologue(): pl.pallas_call(functools.partial(prologue_kernel, levels, sub_count), out...  1.53 us
  transfers between devices with their start and end apart: 10, of which 4 were waited for; matrix products, arithmetic and copies ran while one was open for 0% of the time, Pallas kernels for 12%

profile of v1, /device:TPU:0, one launch (start us, length us, event | category | flops | bytes accessed | tf_op | source)
XLA Modules:
  0.0 38.6 jit_solution(14839071837289109574)
XLA Ops:
  0.0 0.5 %collective-permute-start = (f32[2,256,128]{2,1,0:T(8,128)}, f32[2,256,128]{2,1,0:T(8,128)S(1)}, u32[]{:S(2)}, u32[]{:S(2)}) collective-permute-start(f32[2,256,128]{2,1,0:T(8,128)} %x_hbm.1), channel_id=1, source_target_pairs={{0,1},{1,0},{2,3},{3,2},{4,5},{5,4},{6,7},{7,6},{8,9},{9,8},{10,11... | collective-permute-start | bytes 786440 | tf_op jit(solution)/shard_map/ppermute | solution.py:308
  0.5 1.5 %prologue.1 = (f32[2,256,128]{2,1,0:T(8,128)S(1)}, bf16[2,256,256]{2,1,0:T(8,128)(2,1)S(1)}, bf16[2,256,256]{2,1,0:T(8,128)(2,1)S(1)}, bf16[128,256]{1,0:T(8,128)(2,1)S(1)}, f32[5,6,256,128]{3,2,1,0:T(8,128)S(1)}) custom-call(f32[2,256,128]{2,1,0:T(8,128)} %x_hbm.1, f32[32,128]{1,0:T(8,128)} %bitcast.1, bf16[2,256,256]{2,1,0:T(8,128)(2,1)} %constant.4.clone.even_hbm, ...), custom_call_target="tpu_custom_call" | custom-call | tf_op jit(solution)/shard_map/prologue/pallas_call | solution.py:148
  2.0 0.0 collective-permute-done.far_ref
  2.0 0.4 %shard_map.55 = (f32[2,96,128]{2,1,0:T(8,128)S(1)}, f32[2,80,128]{2,1,0:T(8,128)S(1)}, f32[2,80,128]{2,1,0:T(8,128)S(1)}) custom-call(f32[2,256,128]{2,1,0:T(8,128)S(1)} %get-tuple-element.13.x_ref, f32[2,256,128]{2,1,0:T(8,128)S(1)} %collective-permute-done.far_ref, f32[5,6,256,128]{3,2,1,0:T(8,128)S(1)} %get-tuple-element.14.tab_ref, ...), custom_call_target="tpu_custom_call" | custom-call | tf_op jit(solution)/shard_map/pallas_call | solution.py:196
  2.5 3.8 %collective-permute-start.7 = (f32[2,80,128]{2,1,0:T(8,128)S(1)}, f32[2,80,128]{2,1,0:T(8,128)S(1)}, u32[]{:S(2)}, u32[]{:S(2)}) collective-permute-start(f32[2,80,128]{2,1,0:T(8,128)S(1)} %get-tuple-element.20.a_ref), channel_id=1, source_target_pairs={{0,8},{2,10},{4,12},{6,14},{8,0},{10,2},{12,4},{14,6},{1,9},{3,11}... | collective-permute-start | bytes 245768 | tf_op jit(solution)/shard_map/ppermute | solution.py:308
  6.3 4.7 %collective-permute-done.7.b_ref = f32[2,80,128]{2,1,0:T(8,128)S(1)} collective-permute-done((f32[2,80,128]{2,1,0:T(8,128)S(1)}, f32[2,80,128]{2,1,0:T(8,128)S(1)}, u32[]{:S(2)}, u32[]{:S(2)}) %collective-permute-start.7) | collective-permute-done | bytes 81952 | tf_op jit(solution)/shard_map/ppermute | solution.py:308
  11.0 1.6 %collective-permute-start.8 = (f32[4,80,128]{2,1,0:T(8,128)S(1)}, f32[4,80,128]{2,1,0:T(8,128)S(1)}, u32[]{:S(2)}, u32[]{:S(2)}) collective-permute-start(f32[4,80,128]{2,1,0:T(8,128)S(1)} %shard_map.62.own_ref), channel_id=1, source_target_pairs={{0,2},{2,0},{4,6},{6,4},{8,10},{10,8},{12,14},{14,12},{1,3},{3,1},... | collective-permute-start | bytes 491528 | tf_op jit(solution)/shard_map/ppermute | solution.py:308
  12.6 0.5 %collective-permute-start.1 = (f32[2,96,128]{2,1,0:T(8,128)S(1)}, f32[2,96,128]{2,1,0:T(8,128)S(1)}, u32[]{:S(2)}, u32[]{:S(2)}) collective-permute-start(f32[2,96,128]{2,1,0:T(8,128)S(1)} %get-tuple-element.17.own_ref), channel_id=1, source_target_pairs={{0,2},{2,0},{4,6},{6,4},{8,10},{10,8},{12,14},{14,12},{1,3},{3,1},... | collective-permute-start | bytes 294920 | tf_op jit(solution)/shard_map/ppermute | solution.py:308
  13.1 1.5 %collective-permute-start.4 = (f32[2,80,128]{2,1,0:T(8,128)S(1)}, f32[2,80,128]{2,1,0:T(8,128)S(1)}, u32[]{:S(2)}, u32[]{:S(2)}) collective-permute-start(f32[2,80,128]{2,1,0:T(8,128)S(1)} %get-tuple-element.19.own_ref), channel_id=1, source_target_pairs={{0,2},{2,0},{4,6},{6,4},{8,10},{10,8},{12,14},{14,12},{1,3},{3,1},... | collective-permute-start | bytes 245768 | tf_op jit(solution)/shard_map/ppermute | solution.py:308
  14.6 5.3 %collective-permute-done.1.far_ref = f32[2,96,128]{2,1,0:T(8,128)S(1)} collective-permute-done((f32[2,96,128]{2,1,0:T(8,128)S(1)}, f32[2,96,128]{2,1,0:T(8,128)S(1)}, u32[]{:S(2)}, u32[]{:S(2)}) %collective-permute-start.1) | collective-permute-done | bytes 98336 | tf_op jit(solution)/shard_map/ppermute | solution.py:308
  19.9 0.5 %shard_map.56.own_ref = f32[2,96,128]{2,1,0:T(8,128)S(1)} custom-call(f32[2,96,128]{2,1,0:T(8,128)S(1)} %get-tuple-element.17.own_ref, f32[2,96,128]{2,1,0:T(8,128)S(1)} %collective-permute-done.1.far_ref, f32[5,6,256,128]{3,2,1,0:T(8,128)S(1)} %get-tuple-element.14.tab_ref, bf16[2,256,256]{2,1,0:T(8,128)(2,1)S(1)} %get-tuple-element.18.mat_ref.last_mat_ref, ...), custom_call_target="tpu_custom_call" | custom-call | tf_op jit(solution)/shard_map/pallas_call | solution.py:196
  20.4 1.1 %collective-permute-start.2 = (f32[2,96,128]{2,1,0:T(8,128)S(1)}, f32[2,96,128]{2,1,0:T(8,128)S(1)}, u32[]{:S(2)}, u32[]{:S(2)}) collective-permute-start(f32[2,96,128]{2,1,0:T(8,128)S(1)} %shard_map.56.own_ref), channel_id=1, source_target_pairs={{0,4},{2,6},{4,0},{6,2},{8,12},{10,14},{12,8},{14,10},{1,5},{3,7},... | collective-permute-start | bytes 294920 | tf_op jit(solution)/shard_map/ppermute | solution.py:308
  21.5 0.0 collective-permute-done.4.far_ref
  21.5 0.5 %shard_map.59.own_ref = f32[2,80,128]{2,1,0:T(8,128)S(1)} custom-call(f32[2,80,128]{2,1,0:T(8,128)S(1)} %get-tuple-element.19.own_ref, f32[2,80,128]{2,1,0:T(8,128)S(1)} %collective-permute-done.4.far_ref, f32[5,6,256,128]{3,2,1,0:T(8,128)S(1)} %get-tuple-element.14.tab_ref, bf16[2,256,256]{2,1,0:T(8,128)(2,1)S(1)} %get-tuple-element.18.mat_ref.last_mat_ref, ...), custom_call_target="tpu_custom_call" | custom-call | tf_op jit(solution)/shard_map/pallas_call | solution.py:196
  22.0 1.1 %collective-permute-start.5 = (f32[2,80,128]{2,1,0:T(8,128)S(1)}, f32[2,80,128]{2,1,0:T(8,128)S(1)}, u32[]{:S(2)}, u32[]{:S(2)}) collective-permute-start(f32[2,80,128]{2,1,0:T(8,128)S(1)} %shard_map.59.own_ref), channel_id=1, source_target_pairs={{0,4},{2,6},{4,0},{6,2},{8,12},{10,14},{12,8},{14,10},{1,5},{3,7},... | collective-permute-start | bytes 245768 | tf_op jit(solution)/shard_map/ppermute | solution.py:308
  23.1 0.0 collective-permute-done.8.far_ref
  23.1 0.6 %shard_map.63.own_ref = f32[4,80,128]{2,1,0:T(8,128)S(1)} custom-call(f32[4,80,128]{2,1,0:T(8,128)S(1)} %shard_map.62.own_ref, f32[4,80,128]{2,1,0:T(8,128)S(1)} %collective-permute-done.8.far_ref, f32[5,6,256,128]{3,2,1,0:T(8,128)S(1)} %get-tuple-element.14.tab_ref, bf16[2,256,256]{2,1,0:T(8,128)(2,1)S(1)} %get-tuple-element.18.mat_ref.last_mat_ref, ...), custom_call_target="tpu_custom_call" | custom-call | tf_op jit(solution)/shard_map/pallas_call | solution.py:196
  23.7 1.1 %collective-permute-start.9 = (f32[4,80,128]{2,1,0:T(8,128)S(1)}, f32[4,80,128]{2,1,0:T(8,128)S(1)}, u32[]{:S(2)}, u32[]{:S(2)}) collective-permute-start(f32[4,80,128]{2,1,0:T(8,128)S(1)} %shard_map.63.own_ref), channel_id=1, source_target_pairs={{0,4},{2,6},{4,0},{6,2},{8,12},{10,14},{12,8},{14,10},{1,5},{3,7},... | collective-permute-start | bytes 491528 | tf_op jit(solution)/shard_map/ppermute | solution.py:308
  24.8 0.8 %collective-permute-done.2.far_ref = f32[2,96,128]{2,1,0:T(8,128)S(1)} collective-permute-done((f32[2,96,128]{2,1,0:T(8,128)S(1)}, f32[2,96,128]{2,1,0:T(8,128)S(1)}, u32[]{:S(2)}, u32[]{:S(2)}) %collective-permute-start.2) | collective-permute-done | bytes 98336 | tf_op jit(solution)/shard_map/ppermute | solution.py:308
  25.6 0.3 shard_map.57.own_ref
  26.0 2.6 %collective-permute-start.3 = (f32[2,96,128]{2,1,0:T(8,128)S(1)}, f32[2,96,128]{2,1,0:T(8,128)S(1)}, u32[]{:S(2)}, u32[]{:S(2)}) collective-permute-start(f32[2,96,128]{2,1,0:T(8,128)S(1)} %shard_map.57.own_ref), channel_id=1, source_target_pairs={{0,8},{2,10},{4,12},{6,14},{8,0},{10,2},{12,4},{14,6},{1,9},{3,11}... | collective-permute-start | bytes 294920 | tf_op jit(solution)/shard_map/ppermute | solution.py:308
  28.6 0.0 collective-permute-done.5.far_ref
  28.6 0.3 shard_map.60.own_ref
  28.9 2.2 %collective-permute-start.6 = (f32[2,80,128]{2,1,0:T(8,128)S(1)}, f32[2,80,128]{2,1,0:T(8,128)S(1)}, u32[]{:S(2)}, u32[]{:S(2)}) collective-permute-start(f32[2,80,128]{2,1,0:T(8,128)S(1)} %shard_map.60.own_ref), channel_id=1, source_target_pairs={{0,8},{2,10},{4,12},{6,14},{8,0},{10,2},{12,4},{14,6},{1,9},{3,11}... | collective-permute-start | bytes 245768 | tf_op jit(solution)/shard_map/ppermute | solution.py:308
  31.2 5.3 %collective-permute-done.6.far_ref = f32[2,80,128]{2,1,0:T(8,128)S(1)} collective-permute-done((f32[2,80,128]{2,1,0:T(8,128)S(1)}, f32[2,80,128]{2,1,0:T(8,128)S(1)}, u32[]{:S(2)}, u32[]{:S(2)}) %collective-permute-start.6) | collective-permute-done | bytes 81952 | tf_op jit(solution)/shard_map/ppermute | solution.py:308
  36.5 0.3 shard_map.61.refs_1_
  36.8 0.0 collective-permute-done.3.far_ref
  36.8 0.3 shard_map.58.refs_0_
  37.1 0.0 collective-permute-done.9.far_ref
  37.1 0.7 %shard_map.64.refs_2_ = f32[2,80,128]{2,1,0:T(8,128)S(1)} custom-call(f32[4,80,128]{2,1,0:T(8,128)S(1)} %shard_map.63.own_ref, f32[4,80,128]{2,1,0:T(8,128)S(1)} %collective-permute-done.9.far_ref, f32[5,6,256,128]{3,2,1,0:T(8,128)S(1)} %get-tuple-element.14.tab_ref, bf16[2,256,256]{2,1,0:T(8,128)(2,1)S(1)} %get-tuple-element.15.mat_ref, ...), custom_call_target="tpu_custom_call" | custom-call | tf_op jit(solution)/shard_map/pallas_call | solution.py:196
  37.8 0.7 %shard_map.65 = f32[2,256,128]{2,1,0:T(8,128)} custom-call(f32[2,96,128]{2,1,0:T(8,128)S(1)} %shard_map.58.refs_0_, f32[2,80,128]{2,1,0:T(8,128)S(1)} %shard_map.61.refs_1_, f32[2,80,128]{2,1,0:T(8,128)S(1)} %shard_map.64.refs_2_), custom_call_target="tpu_custom_call" | custom-call | tf_op jit(solution)/shard_map/pallas_call | solution.py:196
  (1 shorter events, 0.0 us)
Async XLA Ops:
  0.0 2.0 %collective-permute-start = (f32[2,256,128]{2,1,0:T(8,128)}, f32[2,256,128]{2,1,0:T(8,128)S(1)}, u32[]{:S(2)}, u32[]{:S(2)}) collective-permute-start(f32[2,256,128]{2,1,0:T(8,128)} %x_hbm.1), channel_id=1, source_target_pairs={{0,1},{1,0},{2,3},{3,2},{4,5},{5,4},{6,7},{7,6},{8,9},{9,8},{10,11... | collective-permute-start | bytes 786440 | tf_op jit(solution)/shard_map/ppermute | solution.py:308
  2.5 8.5 %collective-permute-start.7 = (f32[2,80,128]{2,1,0:T(8,128)S(1)}, f32[2,80,128]{2,1,0:T(8,128)S(1)}, u32[]{:S(2)}, u32[]{:S(2)}) collective-permute-start(f32[2,80,128]{2,1,0:T(8,128)S(1)} %get-tuple-element.20.a_ref), channel_id=1, source_target_pairs={{0,8},{2,10},{4,12},{6,14},{8,0},{10,2},{12,4},{14,6},{1,9},{3,11}... | collective-permute-start | bytes 245768 | tf_op jit(solution)/shard_map/ppermute | solution.py:308
  11.0 12.1 %collective-permute-start.8 = (f32[4,80,128]{2,1,0:T(8,128)S(1)}, f32[4,80,128]{2,1,0:T(8,128)S(1)}, u32[]{:S(2)}, u32[]{:S(2)}) collective-permute-start(f32[4,80,128]{2,1,0:T(8,128)S(1)} %shard_map.62.own_ref), channel_id=1, source_target_pairs={{0,2},{2,0},{4,6},{6,4},{8,10},{10,8},{12,14},{14,12},{1,3},{3,1},... | collective-permute-start | bytes 491528 | tf_op jit(solution)/shard_map/ppermute | solution.py:308
  12.6 7.3 %collective-permute-start.1 = (f32[2,96,128]{2,1,0:T(8,128)S(1)}, f32[2,96,128]{2,1,0:T(8,128)S(1)}, u32[]{:S(2)}, u32[]{:S(2)}) collective-permute-start(f32[2,96,128]{2,1,0:T(8,128)S(1)} %get-tuple-element.17.own_ref), channel_id=1, source_target_pairs={{0,2},{2,0},{4,6},{6,4},{8,10},{10,8},{12,14},{14,12},{1,3},{3,1},... | collective-permute-start | bytes 294920 | tf_op jit(solution)/shard_map/ppermute | solution.py:308
  13.1 8.4 %collective-permute-start.4 = (f32[2,80,128]{2,1,0:T(8,128)S(1)}, f32[2,80,128]{2,1,0:T(8,128)S(1)}, u32[]{:S(2)}, u32[]{:S(2)}) collective-permute-start(f32[2,80,128]{2,1,0:T(8,128)S(1)} %get-tuple-element.19.own_ref), channel_id=1, source_target_pairs={{0,2},{2,0},{4,6},{6,4},{8,10},{10,8},{12,14},{14,12},{1,3},{3,1},... | collective-permute-start | bytes 245768 | tf_op jit(solution)/shard_map/ppermute | solution.py:308
  20.4 5.2 %collective-permute-start.2 = (f32[2,96,128]{2,1,0:T(8,128)S(1)}, f32[2,96,128]{2,1,0:T(8,128)S(1)}, u32[]{:S(2)}, u32[]{:S(2)}) collective-permute-start(f32[2,96,128]{2,1,0:T(8,128)S(1)} %shard_map.56.own_ref), channel_id=1, source_target_pairs={{0,4},{2,6},{4,0},{6,2},{8,12},{10,14},{12,8},{14,10},{1,5},{3,7},... | collective-permute-start | bytes 294920 | tf_op jit(solution)/shard_map/ppermute | solution.py:308
  22.0 6.6 %collective-permute-start.5 = (f32[2,80,128]{2,1,0:T(8,128)S(1)}, f32[2,80,128]{2,1,0:T(8,128)S(1)}, u32[]{:S(2)}, u32[]{:S(2)}) collective-permute-start(f32[2,80,128]{2,1,0:T(8,128)S(1)} %shard_map.59.own_ref), channel_id=1, source_target_pairs={{0,4},{2,6},{4,0},{6,2},{8,12},{10,14},{12,8},{14,10},{1,5},{3,7},... | collective-permute-start | bytes 245768 | tf_op jit(solution)/shard_map/ppermute | solution.py:308
  23.7 13.4 %collective-permute-start.9 = (f32[4,80,128]{2,1,0:T(8,128)S(1)}, f32[4,80,128]{2,1,0:T(8,128)S(1)}, u32[]{:S(2)}, u32[]{:S(2)}) collective-permute-start(f32[4,80,128]{2,1,0:T(8,128)S(1)} %shard_map.63.own_ref), channel_id=1, source_target_pairs={{0,4},{2,6},{4,0},{6,2},{8,12},{10,14},{12,8},{14,10},{1,5},{3,7},... | collective-permute-start | bytes 491528 | tf_op jit(solution)/shard_map/ppermute | solution.py:308
  26.0 10.8 %collective-permute-start.3 = (f32[2,96,128]{2,1,0:T(8,128)S(1)}, f32[2,96,128]{2,1,0:T(8,128)S(1)}, u32[]{:S(2)}, u32[]{:S(2)}) collective-permute-start(f32[2,96,128]{2,1,0:T(8,128)S(1)} %shard_map.57.own_ref), channel_id=1, source_target_pairs={{0,8},{2,10},{4,12},{6,14},{8,0},{10,2},{12,4},{14,6},{1,9},{3,11}... | collective-permute-start | bytes 294920 | tf_op jit(solution)/shard_map/ppermute | solution.py:308
  28.9 7.5 %collective-permute-start.6 = (f32[2,80,128]{2,1,0:T(8,128)S(1)}, f32[2,80,128]{2,1,0:T(8,128)S(1)}, u32[]{:S(2)}, u32[]{:S(2)}) collective-permute-start(f32[2,80,128]{2,1,0:T(8,128)S(1)} %shard_map.60.own_ref), channel_id=1, source_target_pairs={{0,8},{2,10},{4,12},{6,14},{8,0},{10,2},{12,4},{14,6},{1,9},{3,11}... | collective-permute-start | bytes 245768 | tf_op jit(solution)/shard_map/ppermute | solution.py:308

commit v2 on v1

--- a/solution.py
+++ b/solution.py
@@ -13,9 +13,10 @@
 POINTS = CHEB * CHEB
 VEC = 2 * POINTS
 HALF_ROOT = 0.7071067811865476
-SHARES = (6, 5, 5)
+SHARES = (14, 9, 9)
 PLAIN, SPLIT, DOUBLE = range(3)
 KIND = (PLAIN, PLAIN, DOUBLE)
+PENDING = 1
 LANES = 128
 ENTRIES = 6
 VMEM_ROOM = 8 << 20
@@ -111,7 +112,7 @@
         hit = jnp.where(spot == node, 1.0, 0.0)
         spots.append((hit.astype(jnp.bfloat16), (hit * sign).astype(jnp.bfloat16)))
     copies[0].wait()
-    for entry in range(levels + 1):
+    for entry in range(tab_ref.shape[0]):
         level = min(entry, levels - 1)
         code = device % 2 ** (level + 1)
         child = (device // 2**level) % 2
@@ -152,7 +153,7 @@
             jax.ShapeDtypeStruct(mats[0].shape, jnp.bfloat16),
             jax.ShapeDtypeStruct(mats[1].shape, jnp.bfloat16),
             jax.ShapeDtypeStruct((VEC, 2 * VEC), jnp.bfloat16),
-            jax.ShapeDtypeStruct((levels + 1, ENTRIES, tgt, VEC), jnp.float32),
+            jax.ShapeDtypeStruct((levels + (SPLIT in KIND), ENTRIES, tgt, VEC), jnp.float32),
         ],
         in_specs=[anywhere] * 5,
         out_specs=[vmem] * 5,
@@ -216,7 +217,8 @@
         self.switch_level = levels // 2 - 1
         self.src, self.tgt, _ = shape
         total = sum(SHARES)
-        self.widths = [self.tgt * n // total for n in SHARES]
+        self.widths = [self.tgt * n // total for n in SHARES[:-1]]
+        self.widths.append(self.tgt - sum(self.widths))
         self.starts = [sum(self.widths[:c]) for c in range(len(SHARES))]
 
     def far_of(self, value, level):
@@ -263,31 +265,42 @@
     return call(kernel, [kept, received], [(2 * kept.shape[0], *kept.shape[1:])])[0]
 
 
-def early_end(plan, c, own, far, tab, mats, sw):
+def both_levels(plan, c, mine_ref, theirs, own_ref, far_ref, tab_ref, mat_ref, last_mat_ref, sw_ref):
     last = plan.levels - 1
     start = plan.starts[c]
-
-    def kernel(own_ref, far_ref, tab_ref, mat_ref, last_mat_ref, sw_ref, mine_ref, *theirs):
-        x = level_value(plan, last - 1, start, own_ref[...], far_ref[...], tab_ref, mat_ref, sw_ref)
-        half = x.shape[0] // 2
-        mat = last_mat_ref[bit_of(plan.sub_count, last)]
-        for ref in theirs:
-            ref[...] = merged(x[:half], x[half:], tab_ref, last + 1, start, mat)
-        mine_ref[...] = merged(x[:half], x[half:], tab_ref, last, start, mat)
+    x = level_value(plan, last - 1, start, own_ref[...], far_ref[...], tab_ref, mat_ref, sw_ref)
+    half = x.shape[0] // 2
+    mat = last_mat_ref[bit_of(plan.sub_count, last)]
+    for ref in theirs:
+        ref[...] = merged(x[:half], x[half:], tab_ref, last + 1, start, mat)
+    mine_ref[...] = merged(x[:half], x[half:], tab_ref, last, start, mat)
+
+
+def early_end(plan, c, own, *args):
+    def kernel(*refs):
+        both_levels(plan, c, refs[len(args) + 1], refs[len(args) + 2 :], *refs[: len(args) + 1])
 
     shape = (own.shape[0] // 2, *own.shape[1:])
-    return call(kernel, [own, far, tab, mats[(last - 1) % 2], mats[last % 2], sw], [shape] * (1 + (KIND[c] == SPLIT)))
-
-
-def finish(plan, results):
-    flat = [part for result in results for part in result]
+    return call(kernel, [own, *args], [shape] * (1 + (KIND[c] == SPLIT)))
+
+
+def finish(plan, results, pending):
+    flat = [part for result in results for part in result or ()]
+    args = list(flat)
+    if pending is not None:
+        c, *more = pending
+        args += more
+    scratch = [pltpu.SemaphoreType.DMA((len(flat) + 1,))]
+    if pending is not None:
+        shape = (plan.src, plan.widths[c], VEC)
+        scratch.append(pltpu.VMEM(shape, jnp.float32))
 
     def kernel(*refs):
-        parts, out_hbm, sems = list(refs[: len(flat)]), refs[-2], refs[-1]
+        parts, out_hbm, sems = list(refs[: len(flat)]), refs[len(args)], refs[len(args) + 1]
         upper = bit_of(plan.sub_count, plan.levels - 1)
         copies = []
         for start, result in zip(plan.starts, results):
-            for i in range(len(result)):
+            for i in range(len(result or ())):
                 ref = parts.pop(0)
                 rows, count, _ = ref.shape
                 box = 0 if len(result) == 1 else (upper if i == 0 else 1 - upper) * rows
@@ -295,11 +308,17 @@
                 copies.append(pltpu.make_async_copy(ref, place, sems.at[len(copies)]))
         for copy in copies:
             copy.start()
+        if pending is not None:
+            held = refs[-1]
+            own_ref, far_ref, *others = refs[len(flat) : len(args)]
+            held[...] = level_value(plan, plan.levels - 1, plan.starts[c], own_ref[...], far_ref[...], *others)
+            place = out_hbm.at[:, pl.ds(plan.starts[c], plan.widths[c])]
+            copies.append(pltpu.make_async_copy(held, place, sems.at[len(copies)]))
+            copies[-1].start()
         for copy in copies:
             copy.wait()
 
-    scratch = [pltpu.SemaphoreType.DMA((len(flat),))]
-    return call(kernel, flat, [(plan.src, plan.tgt, VEC)], scratch, None, [HBM_SPEC])[0]
+    return call(kernel, args, [(plan.src, plan.tgt, VEC)], scratch, None, [HBM_SPEC])[0]
 
 
 def swapped(value, axis, apart):
@@ -318,21 +337,25 @@
     x, even, odd, sw, tab = prologue(levels, sub_count, box_weights, velocity.reshape(-1, LANES), switch_kernel)
     mats = (even, odd)
     parts = first_step(plan, x, far, tab, mats[0], sw)
-    results = []
+    results, pending = [], None
     for c, (part, *leaving) in enumerate(parts):
         if KIND[c] != PLAIN:
             received = plan.far_of((leaving or [part])[0], last)
             part = join(part, received)
         for level in range(1, levels if KIND[c] == PLAIN else last - 1):
             far = plan.far_of(part, level)
+            if level == last and c == PENDING:
+                pending = (c, part, far, tab, mats[last % 2], sw)
+                break
             part = step(plan, level, c, part, far, tab, mats[level % 2], sw)
         if KIND[c] == PLAIN:
-            results.append((part,))
+            results.append(None if c == PENDING else (part,))
             continue
         far = plan.far_of(part, last - 1)
-        mine, *theirs = early_end(plan, c, part, far, tab, mats, sw)
+        args = (part, far, tab, mats[(last - 1) % 2], mats[last % 2], sw)
+        mine, *theirs = early_end(plan, c, *args)
         results.append((mine, *[plan.far_of(sent, last) for sent in theirs]))
-    return finish(plan, results)
+    return finish(plan, results, pending)
 
 
 def solution(mesh):

time: 38.8 us -> 34.7 us (0.89)
  waiting for transfers between devices: 16.1 us -> 10.8 us
  starting transfers between devices: 16.1 us -> 17.4 us
    ppermute x10, waiting for transfers between devices: 16.1 us -> 10.8 us  [swapped(): return lax.ppermute(value, axis, pairs)]
    ppermute x10, starting transfers between devices: 16.1 us -> 17.4 us  [swapped(): return lax.ppermute(value, axis, pairs)]
    pallas_call x11 -> x10, Pallas kernels: 4.79 us -> 4.73 us  [call(): pl.pallas_call(kernel, out_shape=[jax.ShapeDtypeStruct(s, jnp.float32) fo...]
  transfers between devices with their start and end apart: 10 -> 10, of which waited for: 4 -> 3; matrix products, arithmetic and copies ran while one was open for 0% -> 0% of each run, Pallas kernels for 12% -> 14%
where the time goes in v2:
time: 34.7 us; the launch traced here: 34.5 us
  starting transfers between devices  17.4 us (50%)
  waiting for transfers between devices  10.8 us (31%)
  Pallas kernels  6.16 us (18%)
    ppermute x10, starting transfers between devices, swapped(): return lax.ppermute(value, axis, pairs)  17.4 us
    ppermute x10, waiting for transfers between devices, swapped(): return lax.ppermute(value, axis, pairs)  10.8 us
    pallas_call x10, Pallas kernels, call(): pl.pallas_call(kernel, out_shape=[jax.ShapeDtypeStruct(s, jnp.float32) fo...  4.73 us
    pallas_call x1, Pallas kernels, prologue(): pl.pallas_call(functools.partial(prologue_kernel, levels, sub_count), out...  1.43 us
  transfers between devices with their start and end apart: 10, of which 3 were waited for; matrix products, arithmetic and copies ran while one was open for 0% of the time, Pallas kernels for 14%

profile of v2, /device:TPU:0, one launch (start us, length us, event | category | flops | bytes accessed | tf_op | source)
XLA Modules:
  0.0 34.5 jit_solution(16356963682255080705)
XLA Ops:
  0.0 0.5 %collective-permute-start = (f32[2,256,128]{2,1,0:T(8,128)}, f32[2,256,128]{2,1,0:T(8,128)S(1)}, u32[]{:S(2)}, u32[]{:S(2)}) collective-permute-start(f32[2,256,128]{2,1,0:T(8,128)} %x_hbm.1), channel_id=1, source_target_pairs={{0,1},{1,0},{2,3},{3,2},{4,5},{5,4},{6,7},{7,6},{8,9},{9,8},{10,11... | collective-permute-start | bytes 786440 | tf_op jit(solution)/shard_map/ppermute | solution.py:327
  0.5 1.4 %prologue.1 = (f32[2,256,128]{2,1,0:T(8,128)S(1)}, bf16[2,256,256]{2,1,0:T(8,128)(2,1)S(1)}, bf16[2,256,256]{2,1,0:T(8,128)(2,1)S(1)}, bf16[128,256]{1,0:T(8,128)(2,1)S(1)}, f32[4,6,256,128]{3,2,1,0:T(8,128)S(1)}) custom-call(f32[2,256,128]{2,1,0:T(8,128)} %x_hbm.1, f32[32,128]{1,0:T(8,128)} %bitcast.1, bf16[2,256,256]{2,1,0:T(8,128)(2,1)} %constant.4.clone.even_hbm, ...), custom_call_target="tpu_custom_call" | custom-call | tf_op jit(solution)/shard_map/prologue/pallas_call | solution.py:149
  1.9 0.0 collective-permute-done.far_ref
  1.9 0.4 %shard_map.55 = (f32[2,112,128]{2,1,0:T(8,128)S(1)}, f32[2,72,128]{2,1,0:T(8,128)S(1)}, f32[2,72,128]{2,1,0:T(8,128)S(1)}) custom-call(f32[2,256,128]{2,1,0:T(8,128)S(1)} %get-tuple-element.13.x_ref, f32[2,256,128]{2,1,0:T(8,128)S(1)} %collective-permute-done.far_ref, f32[4,6,256,128]{3,2,1,0:T(8,128)S(1)} %get-tuple-element.14.tab_ref.refs_2_.refs_4_, ...), custom_call_target="tpu_custom_call" | custom-call | tf_op jit(solution)/shard_map/pallas_call | solution.py:197
  2.4 3.9 %collective-permute-start.4 = (f32[2,72,128]{2,1,0:T(8,128)S(1)}, f32[2,72,128]{2,1,0:T(8,128)S(1)}, u32[]{:S(2)}, u32[]{:S(2)}) collective-permute-start(f32[2,72,128]{2,1,0:T(8,128)S(1)} %get-tuple-element.19.a_ref), channel_id=1, source_target_pairs={{0,8},{2,10},{4,12},{6,14},{8,0},{10,2},{12,4},{14,6},{1,9},{3,11}... | collective-permute-start | bytes 221192 | tf_op jit(solution)/shard_map/ppermute | solution.py:327
  6.3 1.5 %collective-permute-start.1 = (f32[2,112,128]{2,1,0:T(8,128)S(1)}, f32[2,112,128]{2,1,0:T(8,128)S(1)}, u32[]{:S(2)}, u32[]{:S(2)}) collective-permute-start(f32[2,112,128]{2,1,0:T(8,128)S(1)} %get-tuple-element.17.own_ref), channel_id=1, source_target_pairs={{0,2},{2,0},{4,6},{6,4},{8,10},{10,8},{12,14},{14,12},{1,3},{3,1},... | collective-permute-start | bytes 344072 | tf_op jit(solution)/shard_map/ppermute | solution.py:327
  7.8 2.7 %collective-permute-done.4.b_ref = f32[2,72,128]{2,1,0:T(8,128)S(1)} collective-permute-done((f32[2,72,128]{2,1,0:T(8,128)S(1)}, f32[2,72,128]{2,1,0:T(8,128)S(1)}, u32[]{:S(2)}, u32[]{:S(2)}) %collective-permute-start.4) | collective-permute-done | bytes 73760 | tf_op jit(solution)/shard_map/ppermute | solution.py:327
  10.5 1.6 %collective-permute-start.5 = (f32[4,72,128]{2,1,0:T(8,128)S(1)}, f32[4,72,128]{2,1,0:T(8,128)S(1)}, u32[]{:S(2)}, u32[]{:S(2)}) collective-permute-start(f32[4,72,128]{2,1,0:T(8,128)S(1)} %shard_map.59.own_ref), channel_id=1, source_target_pairs={{0,2},{2,0},{4,6},{6,4},{8,10},{10,8},{12,14},{14,12},{1,3},{3,1},... | collective-permute-start | bytes 442376 | tf_op jit(solution)/shard_map/ppermute | solution.py:327
  12.2 0.0 collective-permute-done.1.far_ref
  12.2 0.6 %shard_map.56.own_ref = f32[2,112,128]{2,1,0:T(8,128)S(1)} custom-call(f32[2,112,128]{2,1,0:T(8,128)S(1)} %get-tuple-element.17.own_ref, f32[2,112,128]{2,1,0:T(8,128)S(1)} %collective-permute-done.1.far_ref, f32[4,6,256,128]{3,2,1,0:T(8,128)S(1)} %get-tuple-element.14.tab_ref.refs_2_.refs_4_, ...), custom_call_target="tpu_custom_call" | custom-call | tf_op jit(solution)/shard_map/pallas_call | solution.py:197
  12.7 0.8 %collective-permute-start.2 = (f32[2,112,128]{2,1,0:T(8,128)S(1)}, f32[2,112,128]{2,1,0:T(8,128)S(1)}, u32[]{:S(2)}, u32[]{:S(2)}) collective-permute-start(f32[2,112,128]{2,1,0:T(8,128)S(1)} %shard_map.56.own_ref), channel_id=1, source_target_pairs={{0,4},{2,6},{4,0},{6,2},{8,12},{10,14},{12,8},{14,10},{1,5},{3,7},... | collective-permute-start | bytes 344072 | tf_op jit(solution)/shard_map/ppermute | solution.py:327
  13.5 1.5 %collective-permute-start.7 = (f32[2,72,128]{2,1,0:T(8,128)S(1)}, f32[2,72,128]{2,1,0:T(8,128)S(1)}, u32[]{:S(2)}, u32[]{:S(2)}) collective-permute-start(f32[2,72,128]{2,1,0:T(8,128)S(1)} %get-tuple-element.20.own_ref), channel_id=1, source_target_pairs={{0,2},{2,0},{4,6},{6,4},{8,10},{10,8},{12,14},{14,12},{1,3},{3,1},... | collective-permute-start | bytes 221192 | tf_op jit(solution)/shard_map/ppermute | solution.py:327
  15.0 2.9 %collective-permute-done.7.far_ref = f32[2,72,128]{2,1,0:T(8,128)S(1)} collective-permute-done((f32[2,72,128]{2,1,0:T(8,128)S(1)}, f32[2,72,128]{2,1,0:T(8,128)S(1)}, u32[]{:S(2)}, u32[]{:S(2)}) %collective-permute-start.7) | collective-permute-done | bytes 73760 | tf_op jit(solution)/shard_map/ppermute | solution.py:327
  17.8 0.5 %shard_map.62.own_ref = f32[2,72,128]{2,1,0:T(8,128)S(1)} custom-call(f32[2,72,128]{2,1,0:T(8,128)S(1)} %get-tuple-element.20.own_ref, f32[2,72,128]{2,1,0:T(8,128)S(1)} %collective-permute-done.7.far_ref, f32[4,6,256,128]{3,2,1,0:T(8,128)S(1)} %get-tuple-element.14.tab_ref.refs_2_.refs_4_, ...), custom_call_target="tpu_custom_call" | custom-call | tf_op jit(solution)/shard_map/pallas_call | solution.py:197
  18.3 1.4 %collective-permute-start.8 = (f32[2,72,128]{2,1,0:T(8,128)S(1)}, f32[2,72,128]{2,1,0:T(8,128)S(1)}, u32[]{:S(2)}, u32[]{:S(2)}) collective-permute-start(f32[2,72,128]{2,1,0:T(8,128)S(1)} %shard_map.62.own_ref), channel_id=1, source_target_pairs={{0,4},{2,6},{4,0},{6,2},{8,12},{10,14},{12,8},{14,10},{1,5},{3,7},... | collective-permute-start | bytes 221192 | tf_op jit(solution)/shard_map/ppermute | solution.py:327
  19.7 0.0 collective-permute-done.5.far_ref
  19.7 0.6 %shard_map.60.refs_0_ = f32[4,72,128]{2,1,0:T(8,128)S(1)} custom-call(f32[4,72,128]{2,1,0:T(8,128)S(1)} %shard_map.59.own_ref, f32[4,72,128]{2,1,0:T(8,128)S(1)} %collective-permute-done.5.far_ref, f32[4,6,256,128]{3,2,1,0:T(8,128)S(1)} %get-tuple-element.14.tab_ref.refs_2_.refs_4_, bf16[2,256,256]{2,1,0:T(8,128)(2,1)S(1)} %get-tuple-element.18.mat_ref.refs_4_.refs_5_, ...), custom_call_target="tpu_custom_call" | custom-call | tf_op jit(solution)/shard_map/pallas_call | solution.py:197
  20.3 0.8 %collective-permute-start.6 = (f32[4,72,128]{2,1,0:T(8,128)S(1)}, f32[4,72,128]{2,1,0:T(8,128)S(1)}, u32[]{:S(2)}, u32[]{:S(2)}) collective-permute-start(f32[4,72,128]{2,1,0:T(8,128)S(1)} %shard_map.60.refs_0_), channel_id=1, source_target_pairs={{0,4},{2,6},{4,0},{6,2},{8,12},{10,14},{12,8},{14,10},{1,5},{3,7},... | collective-permute-start | bytes 442376 | tf_op jit(solution)/shard_map/ppermute | solution.py:327
  21.1 0.0 collective-permute-done.2.far_ref
  21.1 0.3 %shard_map.57.own_ref = f32[2,112,128]{2,1,0:T(8,128)S(1)} custom-call(f32[2,112,128]{2,1,0:T(8,128)S(1)} %shard_map.56.own_ref, f32[2,112,128]{2,1,0:T(8,128)S(1)} %collective-permute-done.2.far_ref, f32[4,6,256,128]{3,2,1,0:T(8,128)S(1)} %get-tuple-element.14.tab_ref.refs_2_.refs_4_, bf16[2,256,256]{2,1,0:T(8,128)(2,1)S(1)} %get-tuple-element.15.mat_ref.refs_3_, ...), custom_call_target="tpu_custom_call" | custom-call | tf_op jit(solution)/shard_map/pallas_call | solution.py:197
  21.5 3.4 %collective-permute-start.3 = (f32[2,112,128]{2,1,0:T(8,128)S(1)}, f32[2,112,128]{2,1,0:T(8,128)S(1)}, u32[]{:S(2)}, u32[]{:S(2)}) collective-permute-start(f32[2,112,128]{2,1,0:T(8,128)S(1)} %shard_map.57.own_ref), channel_id=1, source_target_pairs={{0,8},{2,10},{4,12},{6,14},{8,0},{10,2},{12,4},{14,6},{1,9},{3,11}... | collective-permute-start | bytes 344072 | tf_op jit(solution)/shard_map/ppermute | solution.py:327
  24.9 0.0 collective-permute-done.8.far_ref
  24.9 0.3 shard_map.63.refs_2_
  25.2 2.1 %collective-permute-start.9 = (f32[2,72,128]{2,1,0:T(8,128)S(1)}, f32[2,72,128]{2,1,0:T(8,128)S(1)}, u32[]{:S(2)}, u32[]{:S(2)}) collective-permute-start(f32[2,72,128]{2,1,0:T(8,128)S(1)} %shard_map.63.refs_2_), channel_id=1, source_target_pairs={{0,8},{2,10},{4,12},{6,14},{8,0},{10,2},{12,4},{14,6},{1,9},{3,11}... | collective-permute-start | bytes 221192 | tf_op jit(solution)/shard_map/ppermute | solution.py:327
  27.3 5.2 %collective-permute-done.3.far_ref = f32[2,112,128]{2,1,0:T(8,128)S(1)} collective-permute-done((f32[2,112,128]{2,1,0:T(8,128)S(1)}, f32[2,112,128]{2,1,0:T(8,128)S(1)}, u32[]{:S(2)}, u32[]{:S(2)}) %collective-permute-start.3) | collective-permute-done | bytes 114720 | tf_op jit(solution)/shard_map/ppermute | solution.py:327
  32.5 0.3 shard_map.58.refs_0_
  32.8 0.0 collective-permute-done.6.refs_1_
  32.8 0.7 %shard_map.61.refs_1_ = f32[2,72,128]{2,1,0:T(8,128)S(1)} custom-call(f32[4,72,128]{2,1,0:T(8,128)S(1)} %shard_map.60.refs_0_, f32[4,72,128]{2,1,0:T(8,128)S(1)} %collective-permute-done.6.refs_1_, f32[4,6,256,128]{3,2,1,0:T(8,128)S(1)} %get-tuple-element.14.tab_ref.refs_2_.refs_4_, bf16[2,256,256]{2,1,0:T(8,128)(2,1)S(1)} %get-tuple-element.15.mat_ref.refs_3_, ...), custom_call_target="tpu_custom_call" | custom-call | tf_op jit(solution)/shard_map/pallas_call | solution.py:197
  33.5 0.0 collective-permute-done.9.refs_3_
  33.5 1.0 %shard_map.64 = f32[2,256,128]{2,1,0:T(8,128)} custom-call(f32[2,112,128]{2,1,0:T(8,128)S(1)} %shard_map.58.refs_0_, f32[2,72,128]{2,1,0:T(8,128)S(1)} %shard_map.61.refs_1_, f32[2,72,128]{2,1,0:T(8,128)S(1)} %shard_map.63.refs_2_, f32[2,72,128]{2,1,0:T(8,128)S(1)} %collective-permute-done.9.refs_3_, ...), custom_call_target="tpu_custom_call" | custom-call | tf_op jit(solution)/shard_map/pallas_call | solution.py:197
  (1 shorter events, 0.0 us)
Async XLA Ops:
  0.0 1.9 %collective-permute-start = (f32[2,256,128]{2,1,0:T(8,128)}, f32[2,256,128]{2,1,0:T(8,128)S(1)}, u32[]{:S(2)}, u32[]{:S(2)}) collective-permute-start(f32[2,256,128]{2,1,0:T(8,128)} %x_hbm.1), channel_id=1, source_target_pairs={{0,1},{1,0},{2,3},{3,2},{4,5},{5,4},{6,7},{7,6},{8,9},{9,8},{10,11... | collective-permute-start | bytes 786440 | tf_op jit(solution)/shard_map/ppermute | solution.py:327
  2.4 8.2 %collective-permute-start.4 = (f32[2,72,128]{2,1,0:T(8,128)S(1)}, f32[2,72,128]{2,1,0:T(8,128)S(1)}, u32[]{:S(2)}, u32[]{:S(2)}) collective-permute-start(f32[2,72,128]{2,1,0:T(8,128)S(1)} %get-tuple-element.19.a_ref), channel_id=1, source_target_pairs={{0,8},{2,10},{4,12},{6,14},{8,0},{10,2},{12,4},{14,6},{1,9},{3,11}... | collective-permute-start | bytes 221192 | tf_op jit(solution)/shard_map/ppermute | solution.py:327
  6.3 5.9 %collective-permute-start.1 = (f32[2,112,128]{2,1,0:T(8,128)S(1)}, f32[2,112,128]{2,1,0:T(8,128)S(1)}, u32[]{:S(2)}, u32[]{:S(2)}) collective-permute-start(f32[2,112,128]{2,1,0:T(8,128)S(1)} %get-tuple-element.17.own_ref), channel_id=1, source_target_pairs={{0,2},{2,0},{4,6},{6,4},{8,10},{10,8},{12,14},{14,12},{1,3},{3,1},... | collective-permute-start | bytes 344072 | tf_op jit(solution)/shard_map/ppermute | solution.py:327
  10.5 9.2 %collective-permute-start.5 = (f32[4,72,128]{2,1,0:T(8,128)S(1)}, f32[4,72,128]{2,1,0:T(8,128)S(1)}, u32[]{:S(2)}, u32[]{:S(2)}) collective-permute-start(f32[4,72,128]{2,1,0:T(8,128)S(1)} %shard_map.59.own_ref), channel_id=1, source_target_pairs={{0,2},{2,0},{4,6},{6,4},{8,10},{10,8},{12,14},{14,12},{1,3},{3,1},... | collective-permute-start | bytes 442376 | tf_op jit(solution)/shard_map/ppermute | solution.py:327
  12.7 8.4 %collective-permute-start.2 = (f32[2,112,128]{2,1,0:T(8,128)S(1)}, f32[2,112,128]{2,1,0:T(8,128)S(1)}, u32[]{:S(2)}, u32[]{:S(2)}) collective-permute-start(f32[2,112,128]{2,1,0:T(8,128)S(1)} %shard_map.56.own_ref), channel_id=1, source_target_pairs={{0,4},{2,6},{4,0},{6,2},{8,12},{10,14},{12,8},{14,10},{1,5},{3,7},... | collective-permute-start | bytes 344072 | tf_op jit(solution)/shard_map/ppermute | solution.py:327
  13.5 4.4 %collective-permute-start.7 = (f32[2,72,128]{2,1,0:T(8,128)S(1)}, f32[2,72,128]{2,1,0:T(8,128)S(1)}, u32[]{:S(2)}, u32[]{:S(2)}) collective-permute-start(f32[2,72,128]{2,1,0:T(8,128)S(1)} %get-tuple-element.20.own_ref), channel_id=1, source_target_pairs={{0,2},{2,0},{4,6},{6,4},{8,10},{10,8},{12,14},{14,12},{1,3},{3,1},... | collective-permute-start | bytes 221192 | tf_op jit(solution)/shard_map/ppermute | solution.py:327
  18.3 6.5 %collective-permute-start.8 = (f32[2,72,128]{2,1,0:T(8,128)S(1)}, f32[2,72,128]{2,1,0:T(8,128)S(1)}, u32[]{:S(2)}, u32[]{:S(2)}) collective-permute-start(f32[2,72,128]{2,1,0:T(8,128)S(1)} %shard_map.62.own_ref), channel_id=1, source_target_pairs={{0,4},{2,6},{4,0},{6,2},{8,12},{10,14},{12,8},{14,10},{1,5},{3,7},... | collective-permute-start | bytes 221192 | tf_op jit(solution)/shard_map/ppermute | solution.py:327
  20.3 12.5 %collective-permute-start.6 = (f32[4,72,128]{2,1,0:T(8,128)S(1)}, f32[4,72,128]{2,1,0:T(8,128)S(1)}, u32[]{:S(2)}, u32[]{:S(2)}) collective-permute-start(f32[4,72,128]{2,1,0:T(8,128)S(1)} %shard_map.60.refs_0_), channel_id=1, source_target_pairs={{0,4},{2,6},{4,0},{6,2},{8,12},{10,14},{12,8},{14,10},{1,5},{3,7},... | collective-permute-start | bytes 442376 | tf_op jit(solution)/shard_map/ppermute | solution.py:327
  21.5 11.0 %collective-permute-start.3 = (f32[2,112,128]{2,1,0:T(8,128)S(1)}, f32[2,112,128]{2,1,0:T(8,128)S(1)}, u32[]{:S(2)}, u32[]{:S(2)}) collective-permute-start(f32[2,112,128]{2,1,0:T(8,128)S(1)} %shard_map.57.own_ref), channel_id=1, source_target_pairs={{0,8},{2,10},{4,12},{6,14},{8,0},{10,2},{12,4},{14,6},{1,9},{3,11}... | collective-permute-start | bytes 344072 | tf_op jit(solution)/shard_map/ppermute | solution.py:327
  25.2 8.3 %collective-permute-start.9 = (f32[2,72,128]{2,1,0:T(8,128)S(1)}, f32[2,72,128]{2,1,0:T(8,128)S(1)}, u32[]{:S(2)}, u32[]{:S(2)}) collective-permute-start(f32[2,72,128]{2,1,0:T(8,128)S(1)} %shard_map.63.refs_2_), channel_id=1, source_target_pairs={{0,8},{2,10},{4,12},{6,14},{8,0},{10,2},{12,4},{14,6},{1,9},{3,11}... | collective-permute-start | bytes 221192 | tf_op jit(solution)/shard_map/ppermute | solution.py:327

commit v3 on v2

--- a/solution.py
+++ b/solution.py
@@ -70,9 +70,9 @@
 
 def mixed_with(x, mat):
     high, low = halves(x)
-    m, n = x.shape[0], mat.shape[1] // 2
-    wide = mm(jnp.concatenate([high, low], 0), mat)
-    return (wide[:m, :n] + wide[m:, :n]) + (wide[:m, n:] + wide[m:, n:])
+    n = mat.shape[1] // 2
+    wide = mm(high, mat)
+    return wide[:, :n] + wide[:, n:] + mm(low, mat[:, :n])
 
 
 def expand(values, spots):

time: 34.7 us -> 34.5 us (level)
  transfers between devices with their start and end apart: 10 -> 10, of which waited for: 3 -> 3; matrix products, arithmetic and copies ran while one was open for 0% -> 0% of each run, Pallas kernels for 14% -> 13%
where the time goes in v3:
time: 34.5 us; the launch traced here: 34.2 us
  starting transfers between devices  17.5 us (51%)
  waiting for transfers between devices  10.7 us (31%)
  Pallas kernels  5.9 us (17%)
    ppermute x10, starting transfers between devices, swapped(): return lax.ppermute(value, axis, pairs)  17.5 us
    ppermute x10, waiting for transfers between devices, swapped(): return lax.ppermute(value, axis, pairs)  10.7 us
    pallas_call x10, Pallas kernels, call(): pl.pallas_call(kernel, out_shape=[jax.ShapeDtypeStruct(s, jnp.float32) fo...  4.47 us
    pallas_call x1, Pallas kernels, prologue(): pl.pallas_call(functools.partial(prologue_kernel, levels, sub_count), out...  1.43 us
  transfers between devices with their start and end apart: 10, of which 3 were waited for; matrix products, arithmetic and copies ran while one was open for 0% of the time, Pallas kernels for 13%

profile of v3, /device:TPU:0, one launch (start us, length us, event | category | flops | bytes accessed | tf_op | source)
XLA Modules:
  0.0 34.2 jit_solution(10959061701221462721)
XLA Ops:
  0.0 0.5 %collective-permute-start = (f32[2,256,128]{2,1,0:T(8,128)}, f32[2,256,128]{2,1,0:T(8,128)S(1)}, u32[]{:S(2)}, u32[]{:S(2)}) collective-permute-start(f32[2,256,128]{2,1,0:T(8,128)} %x_hbm.1), channel_id=1, source_target_pairs={{0,1},{1,0},{2,3},{3,2},{4,5},{5,4},{6,7},{7,6},{8,9},{9,8},{10,11... | collective-permute-start | bytes 786440 | tf_op jit(solution)/shard_map/ppermute | solution.py:327
  0.5 1.4 %prologue.1 = (f32[2,256,128]{2,1,0:T(8,128)S(1)}, bf16[2,256,256]{2,1,0:T(8,128)(2,1)S(1)}, bf16[2,256,256]{2,1,0:T(8,128)(2,1)S(1)}, bf16[128,256]{1,0:T(8,128)(2,1)S(1)}, f32[4,6,256,128]{3,2,1,0:T(8,128)S(1)}) custom-call(f32[2,256,128]{2,1,0:T(8,128)} %x_hbm.1, f32[32,128]{1,0:T(8,128)} %bitcast.1, bf16[2,256,256]{2,1,0:T(8,128)(2,1)} %constant.4.clone.even_hbm, ...), custom_call_target="tpu_custom_call" | custom-call | tf_op jit(solution)/shard_map/prologue/pallas_call | solution.py:149
  1.9 0.0 collective-permute-done.far_ref
  1.9 0.4 %shard_map.55 = (f32[2,112,128]{2,1,0:T(8,128)S(1)}, f32[2,72,128]{2,1,0:T(8,128)S(1)}, f32[2,72,128]{2,1,0:T(8,128)S(1)}) custom-call(f32[2,256,128]{2,1,0:T(8,128)S(1)} %get-tuple-element.13.x_ref, f32[2,256,128]{2,1,0:T(8,128)S(1)} %collective-permute-done.far_ref, f32[4,6,256,128]{3,2,1,0:T(8,128)S(1)} %get-tuple-element.14.tab_ref.refs_2_.refs_4_, ...), custom_call_target="tpu_custom_call" | custom-call | tf_op jit(solution)/shard_map/pallas_call | solution.py:197
  2.4 3.9 %collective-permute-start.4 = (f32[2,72,128]{2,1,0:T(8,128)S(1)}, f32[2,72,128]{2,1,0:T(8,128)S(1)}, u32[]{:S(2)}, u32[]{:S(2)}) collective-permute-start(f32[2,72,128]{2,1,0:T(8,128)S(1)} %get-tuple-element.19.a_ref), channel_id=1, source_target_pairs={{0,8},{2,10},{4,12},{6,14},{8,0},{10,2},{12,4},{14,6},{1,9},{3,11}... | collective-permute-start | bytes 221192 | tf_op jit(solution)/shard_map/ppermute | solution.py:327
  6.3 1.5 %collective-permute-start.1 = (f32[2,112,128]{2,1,0:T(8,128)S(1)}, f32[2,112,128]{2,1,0:T(8,128)S(1)}, u32[]{:S(2)}, u32[]{:S(2)}) collective-permute-start(f32[2,112,128]{2,1,0:T(8,128)S(1)} %get-tuple-element.17.own_ref), channel_id=1, source_target_pairs={{0,2},{2,0},{4,6},{6,4},{8,10},{10,8},{12,14},{14,12},{1,3},{3,1},... | collective-permute-start | bytes 344072 | tf_op jit(solution)/shard_map/ppermute | solution.py:327
  7.8 2.7 %collective-permute-done.4.b_ref = f32[2,72,128]{2,1,0:T(8,128)S(1)} collective-permute-done((f32[2,72,128]{2,1,0:T(8,128)S(1)}, f32[2,72,128]{2,1,0:T(8,128)S(1)}, u32[]{:S(2)}, u32[]{:S(2)}) %collective-permute-start.4) | collective-permute-done | bytes 73760 | tf_op jit(solution)/shard_map/ppermute | solution.py:327
  10.5 1.6 %collective-permute-start.5 = (f32[4,72,128]{2,1,0:T(8,128)S(1)}, f32[4,72,128]{2,1,0:T(8,128)S(1)}, u32[]{:S(2)}, u32[]{:S(2)}) collective-permute-start(f32[4,72,128]{2,1,0:T(8,128)S(1)} %shard_map.59.own_ref), channel_id=1, source_target_pairs={{0,2},{2,0},{4,6},{6,4},{8,10},{10,8},{12,14},{14,12},{1,3},{3,1},... | collective-permute-start | bytes 442376 | tf_op jit(solution)/shard_map/ppermute | solution.py:327
  12.1 0.0 collective-permute-done.1.far_ref
  12.2 0.5 %shard_map.56.own_ref = f32[2,112,128]{2,1,0:T(8,128)S(1)} custom-call(f32[2,112,128]{2,1,0:T(8,128)S(1)} %get-tuple-element.17.own_ref, f32[2,112,128]{2,1,0:T(8,128)S(1)} %collective-permute-done.1.far_ref, f32[4,6,256,128]{3,2,1,0:T(8,128)S(1)} %get-tuple-element.14.tab_ref.refs_2_.refs_4_, ...), custom_call_target="tpu_custom_call" | custom-call | tf_op jit(solution)/shard_map/pallas_call | solution.py:197
  12.6 0.8 %collective-permute-start.2 = (f32[2,112,128]{2,1,0:T(8,128)S(1)}, f32[2,112,128]{2,1,0:T(8,128)S(1)}, u32[]{:S(2)}, u32[]{:S(2)}) collective-permute-start(f32[2,112,128]{2,1,0:T(8,128)S(1)} %shard_map.56.own_ref), channel_id=1, source_target_pairs={{0,4},{2,6},{4,0},{6,2},{8,12},{10,14},{12,8},{14,10},{1,5},{3,7},... | collective-permute-start | bytes 344072 | tf_op jit(solution)/shard_map/ppermute | solution.py:327
  13.4 1.5 %collective-permute-start.7 = (f32[2,72,128]{2,1,0:T(8,128)S(1)}, f32[2,72,128]{2,1,0:T(8,128)S(1)}, u32[]{:S(2)}, u32[]{:S(2)}) collective-permute-start(f32[2,72,128]{2,1,0:T(8,128)S(1)} %get-tuple-element.20.own_ref), channel_id=1, source_target_pairs={{0,2},{2,0},{4,6},{6,4},{8,10},{10,8},{12,14},{14,12},{1,3},{3,1},... | collective-permute-start | bytes 221192 | tf_op jit(solution)/shard_map/ppermute | solution.py:327
  14.9 2.9 %collective-permute-done.7.far_ref = f32[2,72,128]{2,1,0:T(8,128)S(1)} collective-permute-done((f32[2,72,128]{2,1,0:T(8,128)S(1)}, f32[2,72,128]{2,1,0:T(8,128)S(1)}, u32[]{:S(2)}, u32[]{:S(2)}) %collective-permute-start.7) | collective-permute-done | bytes 73760 | tf_op jit(solution)/shard_map/ppermute | solution.py:327
  17.7 0.4 %shard_map.62.own_ref = f32[2,72,128]{2,1,0:T(8,128)S(1)} custom-call(f32[2,72,128]{2,1,0:T(8,128)S(1)} %get-tuple-element.20.own_ref, f32[2,72,128]{2,1,0:T(8,128)S(1)} %collective-permute-done.7.far_ref, f32[4,6,256,128]{3,2,1,0:T(8,128)S(1)} %get-tuple-element.14.tab_ref.refs_2_.refs_4_, ...), custom_call_target="tpu_custom_call" | custom-call | tf_op jit(solution)/shard_map/pallas_call | solution.py:197
  18.2 1.4 %collective-permute-start.8 = (f32[2,72,128]{2,1,0:T(8,128)S(1)}, f32[2,72,128]{2,1,0:T(8,128)S(1)}, u32[]{:S(2)}, u32[]{:S(2)}) collective-permute-start(f32[2,72,128]{2,1,0:T(8,128)S(1)} %shard_map.62.own_ref), channel_id=1, source_target_pairs={{0,4},{2,6},{4,0},{6,2},{8,12},{10,14},{12,8},{14,10},{1,5},{3,7},... | collective-permute-start | bytes 221192 | tf_op jit(solution)/shard_map/ppermute | solution.py:327
  19.6 0.0 collective-permute-done.5.far_ref
  19.6 0.5 %shard_map.60.refs_0_ = f32[4,72,128]{2,1,0:T(8,128)S(1)} custom-call(f32[4,72,128]{2,1,0:T(8,128)S(1)} %shard_map.59.own_ref, f32[4,72,128]{2,1,0:T(8,128)S(1)} %collective-permute-done.5.far_ref, f32[4,6,256,128]{3,2,1,0:T(8,128)S(1)} %get-tuple-element.14.tab_ref.refs_2_.refs_4_, bf16[2,256,256]{2,1,0:T(8,128)(2,1)S(1)} %get-tuple-element.18.mat_ref.refs_4_.refs_5_, ...), custom_call_target="tpu_custom_call" | custom-call | tf_op jit(solution)/shard_map/pallas_call | solution.py:197
  20.1 0.8 %collective-permute-start.6 = (f32[4,72,128]{2,1,0:T(8,128)S(1)}, f32[4,72,128]{2,1,0:T(8,128)S(1)}, u32[]{:S(2)}, u32[]{:S(2)}) collective-permute-start(f32[4,72,128]{2,1,0:T(8,128)S(1)} %shard_map.60.refs_0_), channel_id=1, source_target_pairs={{0,4},{2,6},{4,0},{6,2},{8,12},{10,14},{12,8},{14,10},{1,5},{3,7},... | collective-permute-start | bytes 442376 | tf_op jit(solution)/shard_map/ppermute | solution.py:327
  20.9 0.0 collective-permute-done.2.far_ref
  20.9 0.3 shard_map.57.own_ref
  21.2 3.4 %collective-permute-start.3 = (f32[2,112,128]{2,1,0:T(8,128)S(1)}, f32[2,112,128]{2,1,0:T(8,128)S(1)}, u32[]{:S(2)}, u32[]{:S(2)}) collective-permute-start(f32[2,112,128]{2,1,0:T(8,128)S(1)} %shard_map.57.own_ref), channel_id=1, source_target_pairs={{0,8},{2,10},{4,12},{6,14},{8,0},{10,2},{12,4},{14,6},{1,9},{3,11}... | collective-permute-start | bytes 344072 | tf_op jit(solution)/shard_map/ppermute | solution.py:327
  24.7 0.0 collective-permute-done.8.far_ref
  24.7 0.3 shard_map.63.refs_2_
  25.0 2.1 %collective-permute-start.9 = (f32[2,72,128]{2,1,0:T(8,128)S(1)}, f32[2,72,128]{2,1,0:T(8,128)S(1)}, u32[]{:S(2)}, u32[]{:S(2)}) collective-permute-start(f32[2,72,128]{2,1,0:T(8,128)S(1)} %shard_map.63.refs_2_), channel_id=1, source_target_pairs={{0,8},{2,10},{4,12},{6,14},{8,0},{10,2},{12,4},{14,6},{1,9},{3,11}... | collective-permute-start | bytes 221192 | tf_op jit(solution)/shard_map/ppermute | solution.py:327
  27.1 5.1 %collective-permute-done.3.far_ref = f32[2,112,128]{2,1,0:T(8,128)S(1)} collective-permute-done((f32[2,112,128]{2,1,0:T(8,128)S(1)}, f32[2,112,128]{2,1,0:T(8,128)S(1)}, u32[]{:S(2)}, u32[]{:S(2)}) %collective-permute-start.3) | collective-permute-done | bytes 114720 | tf_op jit(solution)/shard_map/ppermute | solution.py:327
  32.3 0.3 shard_map.58.refs_0_
  32.6 0.0 collective-permute-done.6.refs_1_
  32.6 0.6 %shard_map.61.refs_1_ = f32[2,72,128]{2,1,0:T(8,128)S(1)} custom-call(f32[4,72,128]{2,1,0:T(8,128)S(1)} %shard_map.60.refs_0_, f32[4,72,128]{2,1,0:T(8,128)S(1)} %collective-permute-done.6.refs_1_, f32[4,6,256,128]{3,2,1,0:T(8,128)S(1)} %get-tuple-element.14.tab_ref.refs_2_.refs_4_, bf16[2,256,256]{2,1,0:T(8,128)(2,1)S(1)} %get-tuple-element.15.mat_ref.refs_3_, ...), custom_call_target="tpu_custom_call" | custom-call | tf_op jit(solution)/shard_map/pallas_call | solution.py:197
  33.2 0.0 collective-permute-done.9.refs_3_
  33.3 1.0 %shard_map.64 = f32[2,256,128]{2,1,0:T(8,128)} custom-call(f32[2,112,128]{2,1,0:T(8,128)S(1)} %shard_map.58.refs_0_, f32[2,72,128]{2,1,0:T(8,128)S(1)} %shard_map.61.refs_1_, f32[2,72,128]{2,1,0:T(8,128)S(1)} %shard_map.63.refs_2_, f32[2,72,128]{2,1,0:T(8,128)S(1)} %collective-permute-done.9.refs_3_, ...), custom_call_target="tpu_custom_call" | custom-call | tf_op jit(solution)/shard_map/pallas_call | solution.py:197
  (1 shorter events, 0.0 us)
Async XLA Ops:
  0.0 1.9 %collective-permute-start = (f32[2,256,128]{2,1,0:T(8,128)}, f32[2,256,128]{2,1,0:T(8,128)S(1)}, u32[]{:S(2)}, u32[]{:S(2)}) collective-permute-start(f32[2,256,128]{2,1,0:T(8,128)} %x_hbm.1), channel_id=1, source_target_pairs={{0,1},{1,0},{2,3},{3,2},{4,5},{5,4},{6,7},{7,6},{8,9},{9,8},{10,11... | collective-permute-start | bytes 786440 | tf_op jit(solution)/shard_map/ppermute | solution.py:327
  2.4 8.2 %collective-permute-start.4 = (f32[2,72,128]{2,1,0:T(8,128)S(1)}, f32[2,72,128]{2,1,0:T(8,128)S(1)}, u32[]{:S(2)}, u32[]{:S(2)}) collective-permute-start(f32[2,72,128]{2,1,0:T(8,128)S(1)} %get-tuple-element.19.a_ref), channel_id=1, source_target_pairs={{0,8},{2,10},{4,12},{6,14},{8,0},{10,2},{12,4},{14,6},{1,9},{3,11}... | collective-permute-start | bytes 221192 | tf_op jit(solution)/shard_map/ppermute | solution.py:327
  6.3 5.9 %collective-permute-start.1 = (f32[2,112,128]{2,1,0:T(8,128)S(1)}, f32[2,112,128]{2,1,0:T(8,128)S(1)}, u32[]{:S(2)}, u32[]{:S(2)}) collective-permute-start(f32[2,112,128]{2,1,0:T(8,128)S(1)} %get-tuple-element.17.own_ref), channel_id=1, source_target_pairs={{0,2},{2,0},{4,6},{6,4},{8,10},{10,8},{12,14},{14,12},{1,3},{3,1},... | collective-permute-start | bytes 344072 | tf_op jit(solution)/shard_map/ppermute | solution.py:327
  10.5 9.0 %collective-permute-start.5 = (f32[4,72,128]{2,1,0:T(8,128)S(1)}, f32[4,72,128]{2,1,0:T(8,128)S(1)}, u32[]{:S(2)}, u32[]{:S(2)}) collective-permute-start(f32[4,72,128]{2,1,0:T(8,128)S(1)} %shard_map.59.own_ref), channel_id=1, source_target_pairs={{0,2},{2,0},{4,6},{6,4},{8,10},{10,8},{12,14},{14,12},{1,3},{3,1},... | collective-permute-start | bytes 442376 | tf_op jit(solution)/shard_map/ppermute | solution.py:327
  12.6 8.3 %collective-permute-start.2 = (f32[2,112,128]{2,1,0:T(8,128)S(1)}, f32[2,112,128]{2,1,0:T(8,128)S(1)}, u32[]{:S(2)}, u32[]{:S(2)}) collective-permute-start(f32[2,112,128]{2,1,0:T(8,128)S(1)} %shard_map.56.own_ref), channel_id=1, source_target_pairs={{0,4},{2,6},{4,0},{6,2},{8,12},{10,14},{12,8},{14,10},{1,5},{3,7},... | collective-permute-start | bytes 344072 | tf_op jit(solution)/shard_map/ppermute | solution.py:327
  13.4 4.4 %collective-permute-start.7 = (f32[2,72,128]{2,1,0:T(8,128)S(1)}, f32[2,72,128]{2,1,0:T(8,128)S(1)}, u32[]{:S(2)}, u32[]{:S(2)}) collective-permute-start(f32[2,72,128]{2,1,0:T(8,128)S(1)} %get-tuple-element.20.own_ref), channel_id=1, source_target_pairs={{0,2},{2,0},{4,6},{6,4},{8,10},{10,8},{12,14},{14,12},{1,3},{3,1},... | collective-permute-start | bytes 221192 | tf_op jit(solution)/shard_map/ppermute | solution.py:327
  18.2 6.5 %collective-permute-start.8 = (f32[2,72,128]{2,1,0:T(8,128)S(1)}, f32[2,72,128]{2,1,0:T(8,128)S(1)}, u32[]{:S(2)}, u32[]{:S(2)}) collective-permute-start(f32[2,72,128]{2,1,0:T(8,128)S(1)} %shard_map.62.own_ref), channel_id=1, source_target_pairs={{0,4},{2,6},{4,0},{6,2},{8,12},{10,14},{12,8},{14,10},{1,5},{3,7},... | collective-permute-start | bytes 221192 | tf_op jit(solution)/shard_map/ppermute | solution.py:327
  20.1 12.5 %collective-permute-start.6 = (f32[4,72,128]{2,1,0:T(8,128)S(1)}, f32[4,72,128]{2,1,0:T(8,128)S(1)}, u32[]{:S(2)}, u32[]{:S(2)}) collective-permute-start(f32[4,72,128]{2,1,0:T(8,128)S(1)} %shard_map.60.refs_0_), channel_id=1, source_target_pairs={{0,4},{2,6},{4,0},{6,2},{8,12},{10,14},{12,8},{14,10},{1,5},{3,7},... | collective-permute-start | bytes 442376 | tf_op jit(solution)/shard_map/ppermute | solution.py:327
  21.2 11.0 %collective-permute-start.3 = (f32[2,112,128]{2,1,0:T(8,128)S(1)}, f32[2,112,128]{2,1,0:T(8,128)S(1)}, u32[]{:S(2)}, u32[]{:S(2)}) collective-permute-start(f32[2,112,128]{2,1,0:T(8,128)S(1)} %shard_map.57.own_ref), channel_id=1, source_target_pairs={{0,8},{2,10},{4,12},{6,14},{8,0},{10,2},{12,4},{14,6},{1,9},{3,11}... | collective-permute-start | bytes 344072 | tf_op jit(solution)/shard_map/ppermute | solution.py:327
  25.0 8.3 %collective-permute-start.9 = (f32[2,72,128]{2,1,0:T(8,128)S(1)}, f32[2,72,128]{2,1,0:T(8,128)S(1)}, u32[]{:S(2)}, u32[]{:S(2)}) collective-permute-start(f32[2,72,128]{2,1,0:T(8,128)S(1)} %shard_map.63.refs_2_), channel_id=1, source_target_pairs={{0,8},{2,10},{4,12},{6,14},{8,0},{10,2},{12,4},{14,6},{1,9},{3,11}... | collective-permute-start | bytes 221192 | tf_op jit(solution)/shard_map/ppermute | solution.py:327
